TPU v7x, 256 devices: a whole 4x4x8 slice. The times are simulated.
256 devices in a mesh: mesh: 2 (over y_lo), seq: 8 (over x, core), fsdp: 16 (over z, y_hi).
Axes of the slice: x: 4, y: 4 (y_hi: 2, y_lo: 2; y = y_hi * 2 + y_lo), z: 8, core: 2. Of those that a mesh axis runs over, the one named last changes fastest.
Arguments:
- latents: bfloat16 [16, 512, 5120], P('fsdp', 'mesh'), may hold values from -8 to 8
- noise: bfloat16 [16, 512, 5120], P('fsdp', 'mesh'), may hold values from -6 to 6
- noise_level: float32 [16], P('fsdp'), may hold values from 0.05 to 0.3
- group_index: int32 [16, 512], P('fsdp'), may hold values from 0 to 7, never falling along the last dimension, each value on 1 to 128 neighbouring positions
- projections: bfloat16 [2, 5120, 3, 3072], P('mesh', 'fsdp', None, 'seq'), may hold values from -1 to 1, as said below
- upstream: bfloat16 [16, 512, 3072], P('fsdp', None, 'seq'), may hold values from -0.29882812 to 0.29882812
Outputs:
- direction: bfloat16 [16, 512, 3072], P('fsdp', ('mesh', 'seq'))
- fake_grads: float32 [5120, 3, 3072], P(('mesh', 'fsdp'), None, 'seq')
Inputs may be any that keep to these rules, and one draw needn't show every extreme that they name: `projections`: along the third dimension: query, key and value projection, in that order. `group_index`: along each clip the group numbers never fall; each of the 8 groups holds 1 to 128 tokens.
All inputs are finite; a program needn't handle non-finite values.
Results may differ from a plain program's by a relative error of at most 0.018.
Values may be sent and summed in bfloat16 or wider, within the bound.
A program may use at most 128 MiB of HBM per device.

v0:
```python
import math

import jax
import jax.numpy as jnp
from jax import lax
from jax.sharding import Mesh
from jax.sharding import PartitionSpec as P

HEAD = 128
FSDP = ("fsdp_0", "fsdp_1")
MESH_FSDP = ("mesh", "fsdp_0", "fsdp_1")


def in_one_piece(arrays, axis, dim, along):
    both = jnp.concatenate(arrays, axis=along)
    result, at, done = (lax.all_gather(both, axis, axis=dim, tiled=True), 0, [])
    for a in arrays:
        done.append(lax.slice_in_dim(result, at, at + a.shape[along], axis=along))
        at += a.shape[along]
    return tuple(done)


def cut_along(value, dim, devices):
    before, after = (value.shape[:dim], value.shape[dim + 1 :])
    return jnp.moveaxis(value.reshape(*before, devices, -1, *after), dim, 0)


def sent_and_summed(value, axis, dim):
    devices = lax.axis_size(axis)
    parts = lax.all_to_all(cut_along(value, dim, devices), axis, 0, 0, tiled=True)
    return jnp.sum(parts.astype(jnp.float32), axis=0)


def shifted(value, axis, by):
    devices = lax.axis_size(axis)
    pairs = [(i, i + by) for i in range(devices) if 0 <= i + by < devices]
    return lax.ppermute(value, axis, pairs)


def summed_rows(terms, axes):
    total = terms.astype(jnp.bfloat16)
    for axis in axes:
        total = lax.psum_scatter(total, axis, scatter_dimension=0, tiled=True)
    return total.astype(jnp.float32)


def softmax_parts(queries, key_rows, visible, score_scale):
    scores = (
        jnp.einsum("qhd,khd->hqk", queries, key_rows, preferred_element_type=jnp.float32)
        * score_scale
    )
    scores = jnp.where(visible[None], scores, jnp.float32(-1e30))
    highest = jnp.max(scores, axis=-1, keepdims=True)
    weights = jnp.exp(scores - highest)
    return weights / jnp.sum(weights, axis=-1, keepdims=True)


def contract(columns, factors):
    return lax.dot_general(
        columns, factors, (((0,), (0,)), ((), ())), preferred_element_type=jnp.float32
    )


def per_device(latents, noise, noise_level, group_index, projections, upstream):
    model_index = lax.axis_index("mesh")
    clip_rows, clip_noise = in_one_piece((latents[0], noise[0]), "mesh", 0, 1)
    noise_rate = noise_level[0]
    noised = (
        (1.0 - noise_rate) * clip_rows.astype(jnp.float32)
        + noise_rate * clip_noise.astype(jnp.float32)
    ).astype(jnp.bfloat16)
    length = noised.shape[0]
    head_cols = projections.shape[3]
    head_size = HEAD
    local_heads = head_cols // head_size
    triple_width = 3 * head_cols
    weight_piece = lax.all_gather(projections, FSDP, axis=1, tiled=True)
    row_count = weight_piece.shape[1]
    columns = noised
    projected = jnp.dot(
        columns, weight_piece.reshape(row_count, triple_width), preferred_element_type=jnp.float32
    )
    triple = projected.astype(jnp.bfloat16).reshape(length, 3, local_heads, head_size)
    queries = triple[:, 0]
    key_rows = triple[:, 1]
    values = triple[:, 2]
    groups = group_index[0]
    visible = groups[None, :] <= groups[:, None]
    score_scale = 1.0 / math.sqrt(head_size)
    probabilities = softmax_parts(queries, key_rows, visible, score_scale)
    prob_low = probabilities.astype(jnp.bfloat16)
    attended = jnp.einsum("hqk,khd->qhd", prob_low, values, preferred_element_type=jnp.float32)
    attended = attended.astype(jnp.bfloat16).reshape(length, head_cols)
    model_sign = jnp.where(model_index == 1, 1.0, -1.0).astype(jnp.float32)
    paired = sent_and_summed(
        (model_sign * attended.astype(jnp.float32)).astype(jnp.bfloat16), "mesh", 0
    )
    direction = lax.all_to_all(
        paired.astype(jnp.bfloat16), "seq", split_axis=0, concat_axis=1, tiled=True
    )
    grad_out = upstream[0].reshape(length, local_heads, head_size)
    value_grad = jnp.einsum(
        "hqk,qhd->khd", prob_low, grad_out, preferred_element_type=jnp.float32
    ).astype(jnp.bfloat16)
    prob_grad = jnp.einsum("qhd,khd->hqk", grad_out, values, preferred_element_type=jnp.float32)
    row_inner = jnp.sum(probabilities * prob_grad, axis=-1, keepdims=True)
    score_grad = (probabilities * (prob_grad - row_inner) * score_scale).astype(jnp.bfloat16)
    query_grad = jnp.einsum(
        "hqk,khd->qhd", score_grad, key_rows, preferred_element_type=jnp.float32
    ).astype(jnp.bfloat16)
    key_grad = jnp.einsum(
        "hqk,qhd->khd", score_grad, queries, preferred_element_type=jnp.float32
    ).astype(jnp.bfloat16)
    cotangents = jnp.stack([query_grad, key_grad, value_grad], axis=1).reshape(length, triple_width)
    shard_rows = projections.shape[1] // lax.axis_size("mesh")
    received = shifted(cotangents, "mesh", -1)
    fake_side = jnp.where(model_index == 1, cotangents, received)
    offset = model_index * (noised.shape[1] // lax.axis_size("mesh"))
    columns = lax.dynamic_slice_in_dim(noised, offset, shard_rows * lax.axis_size(FSDP), 1)
    summed = summed_rows(contract(columns, fake_side), FSDP)
    return (direction[None], summed.reshape(shard_rows, 3, head_cols))


def solution(mesh):
    split = Mesh(
        mesh.devices.reshape(mesh.shape["mesh"], mesh.shape["seq"], 8, 2),
        ("mesh", "seq", "fsdp_0", "fsdp_1"),
    )
    return jax.shard_map(
        per_device,
        mesh=split,
        in_specs=(
            P(FSDP, "mesh", None),
            P(FSDP, "mesh", None),
            P(FSDP),
            P(FSDP, None),
            P("mesh", FSDP, None, "seq"),
            P(FSDP, None, "seq"),
        ),
        out_specs=(P(FSDP, ("mesh", "seq"), None), P(MESH_FSDP, None, "seq")),
        check_vma=False,
    )
```

profile of v0, /device:TPU:1, one launch (start us, length us, event | category | flops | bytes accessed | tf_op | source)
XLA Modules:
  0.0 507.7 jit_solution(16012796274964791925)
XLA Ops:
  7.2 0.0 all-gather.3.cloned.1.call-start
  7.2 5.4 %pad_maximum_fusion = bf16[256,10240]{1,0:T(8,128)(2,1)} fusion(bf16[256,5120]{1,0:T(8,128)(2,1)} %bitcast.95, bf16[256,5120]{1,0:T(8,128)(2,1)} %bitcast.96), kind=kLoop, calls=%fused_computation.4 | loop fusion | flops 10485760 | bytes 10485760 | tf_op jit(solution)/shard_map/concatenate | solution.py:15
  12.6 0.0 copy-start
  12.6 0.0 copy-start.1
  12.6 0.0 all-gather.3.cloned.1.call-update
  12.6 0.0 all-gather.5.cloned.1.call-start
  12.7 0.7 all-gather.5.cloned.1.call-update
  13.4 0.0 reduce-scatter.3.cloned.1.call-start
  14.1 0.0 copy-done
  14.1 0.2 copy.59
  14.3 0.0 copy-done.1
  14.3 0.2 broadcast_compare_fusion
  14.5 136.5 %all-gather.3.cloned.1.call-done = bf16[512,10240]{1,0:T(8,128)(2,1)} async-done(((bf16[256,10240]{1,0:T(8,128)(2,1)}), bf16[512,10240]{1,0:T(8,128)(2,1)}) %all-gather.3.cloned.1.call-update) | async-done | bytes 10485776 | tf_op jit(solution)/shard_map/all_gather | solution.py:16
  151.0 8.5 %add_convert_fusion = bf16[512,5120]{1,0:T(8,128)(2,1)} fusion(bf16[512,10240]{1,0:T(8,128)(2,1)} %all-gather.3.cloned.1.call-done, f32[]{:T(128)} %bitcast.87, f32[]{:T(128)S(6)} %sub.19), kind=kLoop, calls=%fused_computation.3 | loop fusion | flops 15728640 | bytes 15728648 | tf_op jit(solution)/shard_map/convert_element_type | solution.py:71
  159.5 164.4 %all-gather.5.cloned.1.call-done = bf16[1,5120,3,384]{3,1,2,0:T(8,128)(2,1)} async-done(((bf16[1,320,3,384]{3,1,2,0:T(8,128)(2,1)}), bf16[1,5120,3,384]{3,1,2,0:T(8,128)(2,1)}) %all-gather.5.cloned.1.call-update) | async-done | bytes 11796496 | tf_op jit(solution)/shard_map/all_gather | solution.py:77
  323.9 15.0 %copy.50 = bf16[1,5120,3,384]{1,3,2,0:T(8,128)(2,1)} copy(bf16[1,5120,3,384]{3,1,2,0:T(8,128)(2,1)} %all-gather.5.cloned.1.call-done) | data formatting | bytes 23592960 | tf_op jit(solution)/shard_map/all_gather | solution.py:77
  338.9 10.8 %convolution_convert_fusion.1 = bf16[512,1152]{1,0:T(8,128)(2,1)S(1)} fusion(bf16[512,5120]{1,0:T(8,128)(2,1)} %add_convert_fusion, bf16[5120,1152]{0,1:T(8,128)(2,1)} %bitcast.88), kind=kOutput, calls=%fused_computation.12 | convolution fusion | flops 6040387584 | bytes 18219008 | tf_op jit(solution)/shard_map/dot_general | solution.py:80
  349.7 0.6 copy.51
  350.3 0.6 fusion.27
  350.9 2.3 fusion.26
  353.2 1.7 fusion.35
  354.9 0.0 copy-start.2
  354.9 1.7 copy-done.2
  356.6 0.7 fusion.18
  357.3 6.1 %fusion.21 = bf16[512,1,3,128]{0,3,2,1:T(8,128)(2,1)S(1)} fusion(f32[3,512,512]{2,1,0:T(8,128)} %fusion.26, bf16[512,3,3,128]{0,3,2,1:T(8,128)(2,1)S(1)} %bitcast.91, f32[3,512,512]{1,2,0:T(8,128)} %copy-done.2, f32[3,512]{1,0:T(4,128)S(1)} %get-tuple-element.10), kind=kOutput, calls=%fused_computation.32 | convolution fusion | flops 207030272 | bytes 13385728 | tf_op jit(solution)/shard_map/hqk,khd->qhd/dot_general | solution.py:108
  363.4 5.9 %fusion.20 = bf16[512,1,3,128]{0,3,2,1:T(8,128)(2,1)S(1)} fusion(f32[3,512,512]{2,1,0:T(8,128)} %fusion.26, bf16[512,3,3,128]{0,3,2,1:T(8,128)(2,1)S(1)} %bitcast.92, f32[3,512,512]{1,2,0:T(8,128)} %copy-done.2, f32[3,512]{1,0:T(4,128)S(1)} %get-tuple-element.10), kind=kOutput, calls=%fused_computation.31 | convolution fusion | flops 207030272 | bytes 13385728 | tf_op jit(solution)/shard_map/hqk,qhd->khd/dot_general | solution.py:111
  369.3 0.1 pad_maximum_fusion.1
  369.5 1.5 collective-permute-start
  370.9 26.5 %collective-permute-done = bf16[512,1152]{0,1:T(8,128)(2,1)S(1)} collective-permute-done((bf16[512,1152]{0,1:T(8,128)(2,1)S(1)}, bf16[512,1152]{0,1:T(8,128)(2,1)S(1)}, u32[]{:S(2)}, u32[]{:S(2)}) %collective-permute-start) | collective-permute-done | bytes 1179680 | tf_op jit(solution)/shard_map/ppermute | solution.py:37
  397.5 7.9 %convolution_convert_fusion = bf16[2560,1152]{1,0:T(8,128)(2,1)} fusion(bf16[512,5120]{1,0:T(8,128)(2,1)} %add_convert_fusion, s32[]{:T(128)S(6)} %select_n.21, bf16[512,1152]{0,1:T(8,128)(2,1)S(1)} %bitcast.100, bf16[512,1152]{0,1:T(8,128)(2,1)S(1)} %collective-permute-done, pred[]{:T(512)S(6)} %eq.4), kind=kOutput, calls=%fused_computation.2 | convolution fusion | flops 3023437824 | bytes 10878981 | tf_op jit(solution)/shard_map/dot_general | solution.py:59
  405.4 0.0 reduce-scatter.3.cloned.1.call-update
  405.4 0.0 reduce-scatter.5.cloned.1.call-start
  405.4 69.2 %reduce-scatter.3.cloned.1.call-done = bf16[320,1152]{1,0:T(8,128)(2,1)} async-done(((bf16[2560,1152]{1,0:T(8,128)(2,1)}), bf16[320,1152]{1,0:T(8,128)(2,1)}) %reduce-scatter.3.cloned.1.call-update) | async-done | bytes 737296 | tf_op jit(solution)/shard_map/reduce_scatter | solution.py:43
  474.7 0.0 reduce-scatter.5.cloned.1.call-update
  474.7 2.3 fusion.19
  477.0 0.1 convert_element_type.71
  477.1 8.2 %all_to_all.21 = bf16[2,256,384]{1,2,0:T(8,128)(2,1)S(1)} all-to-all(bf16[2,256,384]{1,2,0:T(8,128)(2,1)S(1)} %copy.55), channel_id=1, replica_groups=mesh['mesh'=2,'seq'=8,'fsdp_0'=8,'fsdp_1'=2] {'mesh'}, dimensions={0} | all-to-all | bytes 786432 | tf_op jit(solution)/shard_map/all_to_all | solution.py:30
  485.3 0.1 reduce_sum.31
  485.4 0.2 copy.57
  485.5 12.1 %all_to_all.22 = bf16[8,32,384]{2,1,0:T(8,128)(2,1)S(1)} all-to-all(bf16[8,32,384]{2,1,0:T(8,128)(2,1)S(1)} %bitcast.101), channel_id=1, replica_groups=mesh['mesh'=2,'seq'=8,'fsdp_0'=8,'fsdp_1'=2] {'seq'}, dimensions={0} | all-to-all | bytes 393216 | tf_op jit(solution)/shard_map/all_to_all | solution.py:98
  497.6 0.1 copy.58
  497.7 0.8 broadcast_in_dim.21
  498.4 0.8 reduce-scatter.5.cloned.1.call-done
  499.2 1.0 reshape.68
  500.2 0.9 copy.81
  (1 shorter events, 0.0 us)
Async XLA Ops:
  7.2 143.8 %all-gather.3.cloned.1.call-start = ((), (), s32[]{:S(2)}) async-start(), calls=%async_computation.4 | async-start | bytes 15728640 | tf_op jit(solution)/shard_map/all_gather | solution.py:16
  12.6 1.5 copy-start
  12.6 1.7 copy-start.1
  12.6 311.3 %all-gather.5.cloned.1.call-start = ((), (), s32[]{:S(2)}) async-start(), calls=%async_computation.5 | async-start | bytes 12533760 | tf_op jit(solution)/shard_map/all_gather | solution.py:77
  13.4 461.3 %reduce-scatter.3.cloned.1.call-start = ((), (), s32[]{:S(2)}) async-start(), calls=%async_computation.6 | async-start | bytes 6635520 | tf_op jit(solution)/shard_map/reduce_scatter | solution.py:43
  354.9 1.7 copy-start.2
  369.5 28.0 %collective-permute-start = (bf16[512,1152]{0,1:T(8,128)(2,1)S(1)}, bf16[512,1152]{0,1:T(8,128)(2,1)S(1)}, u32[]{:S(2)}, u32[]{:S(2)}) collective-permute-start(bf16[512,1152]{0,1:T(8,128)(2,1)S(1)} %bitcast.99), channel_id=1, source_target_pairs={{128,0},{129,1},{130,2},{131,3},{132,4},{133,5},{134,6},{135,7},{1... | collective-permute-start | bytes 3538952 | tf_op jit(solution)/shard_map/ppermute | solution.py:37
  405.4 93.8 %reduce-scatter.5.cloned.1.call-start = ((), (), s32[]{:S(2)}) async-start(), calls=%async_computation.7 | async-start | bytes 1105920 | tf_op jit(solution)/shard_map/reduce_scatter | solution.py:43
Sparse Core Ops, SparseCore 0:
  12.7 138.1 all-gather.2
  153.6 170.2 all-gather.4
  405.5 69.1 reduce-scatter.2
  477.0 22.1 reduce-scatter.4
where the time goes:
time: 508 us
  waiting for transfers between devices  398 us (78%)
  matrix products  36.5 us (7%)
  blocking collectives  20.2 us (4%)
  local copies, waits for them, and re-layouts  19.6 us (4%)
  other arithmetic  17.1 us (3%)
  between operations  14.6 us (3%)
    all_gather x1, waiting for transfers between devices, per_device(): weight_piece = lax.all_gather(projections, FSDP, axis=1, tiled=True)  164 us
    all_gather x1, waiting for transfers between devices, in_one_piece(): result, at, done = (lax.all_gather(both, axis, axis=dim, tiled=True), 0, [])  136 us
    reduce_scatter x2, waiting for transfers between devices, summed_rows(): total = lax.psum_scatter(total, axis, scatter_dimension=0, tiled=True)  70 us
    ppermute x1, waiting for transfers between devices, shifted(): return lax.ppermute(value, axis, pairs)  26.5 us
    all_gather x1, local copies, waits for them, and re-layouts, per_device(): weight_piece = lax.all_gather(projections, FSDP, axis=1, tiled=True)  15 us
    all_to_all x1, blocking collectives, per_device(): lax.all_to_all(paired.astype(jnp.bfloat16), 'seq', split_axis=0, concat_a...  12.1 us
    dot_general x1, matrix products, per_device(): jnp.dot(columns, weight_piece.reshape(row_count, triple_width), preferred...  10.8 us
  transfers between devices with their start and end apart: 5, of which 5 were waited for; matrix products, arithmetic and copies ran while one was open for 2% of the time, Pallas kernels for 0%

commit v1 on v0

v1 whole, which is shorter than its diff:
```python
import math

import jax
import jax.numpy as jnp
from jax import lax
from jax.experimental import pallas as pl
from jax.experimental.pallas import tpu as pltpu
from jax.sharding import Mesh
from jax.sharding import PartitionSpec as P

HEAD = 128
AXES = ("m", "x", "c", "z", "yh")
MESH_ID = pl.DeviceIdType.MESH
F32 = jnp.float32
BF16 = jnp.bfloat16
OFFSETS = (0, -1, 1, -2, 2, -3, 3, 4)
GROUP_ORDER = (1, 2, 0)


def dot(a, b, dims):
    return lax.dot_general(a, b, (dims, ((), ())), preferred_element_type=F32)


def step_kernel(
    lat_ref, noi_ref, lvl_ref, proj_ref, up_ref, gi_ref,
    dir_ref, grad_ref,
    wbuf, xbuf, latv, noiv, acc, tri, upb, gib, gcol, attb, cotb, coto,
    xts, xto, pbuf, dsbuf, gbuf, sbuf, rbuf, fbuf, obuf, dbuf,
    wr, wc, ws, wcs, wos, xr, xs, lsem, usem, xtr, xtss, cr, cs, er, es,
    rr, rs, fr, fs, dr, dsm,
):
    m, x, c, z, yh = (lax.axis_index(a) for a in AXES)
    nz = lax.axis_size("z")
    nx = lax.axis_size("x")
    home = c == yh
    away = c != yh

    def at(**k):
        return k

    core_p = at(c=1 - c)
    sib = at(m=1 - m)
    out = at(m=1 - m, yh=1 - yh)
    turn = at(c=yh, yh=c)
    up_z = at(z=lax.rem(z + 1, nz))
    dn_z = at(z=lax.rem(z + nz - 1, nz))
    blk = [lax.rem(z + nz + o, nz) for o in OFFSETS]

    def rcopy(src, dst, ss, rsem, dev):
        return pltpu.make_async_remote_copy(
            src_ref=src, dst_ref=dst, send_sem=ss, recv_sem=rsem,
            device_id=dev, device_id_type=MESH_ID,
        )

    def wait_on(ref, sem):
        pltpu.make_async_copy(ref, ref, sem).wait()

    pending = []

    def send(cp, cond=None):
        if cond is None:
            cp.start()
        else:
            pl.when(cond)(cp.start)
        pending.append((cp, cond))

    rows_m = pl.ds(pl.multiple_of(m * 256, 256), 256)
    rows_o = pl.ds(pl.multiple_of((1 - m) * 256, 256), 256)

    def lane(k):
        return pl.ds(pl.multiple_of(blk[k] * 640, 128), 640)

    def read(k, which):
        src, dst = ((lat_ref, latv), (noi_ref, noiv))[which]
        return pltpu.make_async_copy(src.at[:, lane(k)], dst.at[k], lsem.at[k, which])

    w_half = [pl.ds(pl.multiple_of(c * 320 + 160 * i, 16), 160) for i in range(2)]
    w_home = [pl.ds(pl.multiple_of(yh * 320 + 160 * i, 16), 160) for i in range(2)]

    @pl.when(home)
    def _():
        for i in range(2):
            for j in range(3):
                pltpu.make_async_copy(
                    proj_ref.at[j, pl.ds(160 * i, 160), :],
                    wbuf.at[z, w_home[i], pl.ds(384 * j, 384)], wr.at[0, i],
                ).start()
        for k in range(8):
            read(k, 0).start()
            read(k, 1).start()

    barrier = pltpu.get_barrier_semaphore()
    count = 0
    for dm in range(2):
        for dx in range(4):
            for dc in range(2):
                for dy in range(2):
                    if dm + dx + dc + dy == 0:
                        continue
                    peer = at(
                        m=lax.rem(m + dm, 2), x=lax.rem(x + dx, nx),
                        c=lax.rem(c + dc, 2), yh=lax.rem(yh + dy, 2),
                    )
                    pl.semaphore_signal(barrier, inc=1, device_id=peer, device_id_type=MESH_ID)
                    count += 1
    for peer in (up_z, dn_z):
        pl.semaphore_signal(barrier, inc=1, device_id=peer, device_id_type=MESH_ID)
        count += 1
    pl.semaphore_wait(barrier, count)

    for i in range(2):
        for j in range(3):
            send(
                rcopy(
                    proj_ref.at[j, pl.ds(160 * i, 160), :],
                    wbuf.at[z, w_home[i], pl.ds(384 * j, 384)],
                    wos.at[i, j], wr.at[0, i], turn,
                ),
                away,
            )
    send(rcopy(gi_ref, gib, usem.at[2], usem.at[3], turn), away)
    up_keep = jnp.logical_or(home, m == 0)
    up_move = jnp.logical_and(away, m == 1)
    send(rcopy(up_ref, upb, usem.at[0], usem.at[1], turn), up_move)

    @pl.when(up_keep)
    def _():
        pltpu.make_async_copy(up_ref, upb, usem.at[1]).start()

    @pl.when(home)
    def _():
        pltpu.make_async_copy(gi_ref, gib, usem.at[3]).start()

    rate = lvl_ref[0]

    def noise(k):
        @pl.when(home)
        def _():
            read(k, 0).wait()
            read(k, 1).wait()
            xbuf[blk[k], rows_m, :] = (
                (1.0 - rate) * latv[k].astype(F32) + rate * noiv[k].astype(F32)
            ).astype(BF16)

    def x_own(k):
        piece = xbuf.at[blk[k], rows_m, :]
        send(rcopy(piece, piece, xs.at[0, k], xr.at[0, k], sib), home)
        send(rcopy(piece, piece, xs.at[1, k], xr.at[1, k], out), home)

    def x_event(k):
        piece = xbuf.at[blk[k], rows_o, :]

        @pl.when(home)
        def _():
            wait_on(piece, xr.at[0, k])

        @pl.when(away)
        def _():
            wait_on(piece, xr.at[1, k])

        if k % 2 == 1:
            send(rcopy(piece, piece, xs.at[2, k], xr.at[2, k], out), home)
        else:
            send(rcopy(piece, piece, xs.at[2, k], xr.at[2, k], sib), away)
        if k + 4 < 8:
            noise(k + 4)
        if k + 3 < 8:
            x_own(k + 3)

    def w_event(k, i):
        piece = wbuf.at[blk[k], w_half[i], :]
        wait_on(piece, wr.at[k, i])
        o = OFFSETS[k]
        if -3 < o <= 0 or (o == -3 and i == 0):
            send(rcopy(piece, piece, ws.at[0, k, i], wr.at[OFFSETS.index(o - 1 if o > -3 else 4), i], up_z))
        if 0 <= o < 3 or (o == 3 and i == 1):
            send(rcopy(piece, piece, ws.at[1, k, i], wr.at[OFFSETS.index(o + 1), i], dn_z))
        send(rcopy(piece, piece, wcs.at[k, i], wc.at[k, i], core_p))

    w_other = [pl.ds(pl.multiple_of((1 - c) * 320 + 160 * i, 16), 160) for i in range(2)]

    def multiply(k):
        for i in range(2):
            wait_on(wbuf.at[blk[k], w_other[i], :], wc.at[k, i])

        @pl.when(away)
        def _():
            wait_on(xbuf.at[blk[k], rows_m, :], xr.at[2, k])

        for lo, hi in ((0, 640), (640, 1152)):
            part = dot(xbuf[blk[k]], wbuf[blk[k], :, lo:hi], ((1,), (0,)))
            if k == 0:
                acc[:, lo:hi] = part
            else:
                acc[:, lo:hi] += part

    def turned(k):
        @pl.when(blk[k] // 4 == m)
        def _():
            base = lax.rem(blk[k], 4) * 320
            for i in range(5):
                t = xbuf[blk[k], :, i * 128 : (i + 1) * 128].T
                r = i * 128
                while r < (i + 1) * 128:
                    end = min((i + 1) * 128, (r // 160 + 1) * 160)
                    first = pl.multiple_of(base + (r // 320) * 160 + r % 160, 16)
                    xts[(r % 320) // 160, pl.ds(first, end - r), :] = t[r - i * 128 : end - i * 128, :]
                    r = end

    def turned_send(k):
        span = pl.ds(pl.multiple_of(lax.rem(blk[k], 4) * 320, 16), 320)
        q = lax.rem(blk[k], 4)
        send(
            rcopy(xts.at[1 - c, span, :], xto.at[span, :], xtss.at[q], xtr.at[q], core_p),
            blk[k] // 4 == m,
        )

    noise(0)
    noise(1)
    x_own(0)
    noise(2)
    x_own(1)
    noise(3)
    x_own(2)
    w_event(0, 0)
    w_event(0, 1)
    x_event(0)
    x_event(1)
    w_event(1, 0)
    w_event(2, 0)
    x_event(2)
    w_event(1, 1)
    w_event(2, 1)
    multiply(0)
    turned(0)
    x_event(3)
    w_event(3, 0)
    w_event(4, 0)
    multiply(1)
    turned_send(0)
    turned(1)
    x_event(4)
    w_event(3, 1)
    w_event(4, 1)
    multiply(2)
    turned_send(1)
    turned(2)
    x_event(5)
    w_event(5, 0)
    w_event(6, 0)
    multiply(3)
    turned_send(2)
    turned(3)
    x_event(6)
    w_event(5, 1)
    w_event(6, 1)
    multiply(4)
    turned_send(3)
    turned(4)
    x_event(7)
    multiply(5)
    turned_send(4)
    turned(5)
    multiply(6)
    turned_send(5)
    turned(6)
    w_event(7, 0)
    w_event(7, 1)
    multiply(7)
    turned_send(6)
    turned(7)
    tri[...] = acc[...].astype(BF16)
    turned_send(7)

    wait_on(gib, usem.at[3])
    wait_on(upb, usem.at[1])
    gcol[...] = jnp.transpose(jnp.broadcast_to(gib[0:1, :], (128, 512)))
    scale = 1.0 / math.sqrt(HEAD)
    fake = m == 1
    for h in range(3):
        qc, kc, vc = (pl.ds(j * 384 + h * 128, 128) for j in range(3))
        hc = pl.ds(h * 128, 128)
        for b in range(4):
            nk = min(512, (b + 2) * 128)
            rows = pl.ds(b * 128, 128)
            s = dot(tri[rows, qc], tri[0:nk, kc], ((1,), (1,))) * scale
            mine = gcol[rows, :]
            visible = gib[0:1, 0:nk] <= jnp.concatenate([mine] * (nk // 128), axis=1)
            s = jnp.where(visible, s, F32(-1e30))
            w = jnp.exp(s - jnp.max(s, axis=-1, keepdims=True))
            p = w * (1.0 / jnp.sum(w, axis=-1, keepdims=True))
            low = p.astype(BF16)
            attb[rows, hc] = dot(low, tri[0:nk, vc], ((1,), (0,))).astype(BF16)

            @pl.when(fake)
            def _():
                dp = dot(upb[rows, hc], tri[0:nk, vc], ((1,), (1,)))
                inner = jnp.sum(p * dp, axis=-1, keepdims=True)
                ds = (p * (dp - inner) * scale).astype(BF16)
                cotb[rows, qc] = dot(ds, tri[0:nk, kc], ((1,), (0,))).astype(BF16)
                pbuf[rows, 0:nk] = low
                dsbuf[rows, 0:nk] = ds

        @pl.when(fake)
        def _():
            for b in range(4):
                first = max(0, (b - 1) * 128)
                rows = pl.ds(first, 512 - first)
                keys = pl.ds(b * 128, 128)
                cotb[keys, vc] = dot(pbuf[rows, keys], upb[rows, hc], ((0,), (0,))).astype(BF16)
                cotb[keys, kc] = dot(dsbuf[rows, keys], tri[rows, qc], ((0,), (0,))).astype(BF16)

    parts = (
        (pl.ds(384, 256), sib),
        (pl.ds(640, 128), out),
        (pl.ds(768, 384), out),
        (pl.ds(0, 384), sib),
    )
    for n, (cols, peer) in enumerate(parts):
        piece = cotb.at[:, cols]
        send(rcopy(piece, piece, cs.at[n], cr.at[n], peer), fake)

    mine_cols = pl.ds(pl.multiple_of((x * 2 + yh) * 384, 128), 384)
    for dm in range(2):
        for dx in range(4):
            for dc in range(2):
                tm, tx, tc = lax.rem(m + dm, 2), lax.rem(x + dx, nx), lax.rem(c + dc, 2)
                src = attb.at[pl.ds(pl.multiple_of((tm * 8 + tx * 2 + tc) * 32, 32), 32), :]
                dst = dbuf.at[m, :, mine_cols]
                sem = dr.at[dm, dx, yh]
                cp = rcopy(src, dst, dsm.at[dm, dx, dc], sem, at(m=tm, x=tx, c=tc, yh=c))
                if dm + dx + dc == 0:
                    send(cp, away)

                    @pl.when(home)
                    def _():
                        pltpu.make_async_copy(src, dst, sem).start()
                else:
                    send(cp)

    def exchange(g):
        piece = cotb.at[:, pl.ds(g * 384, 384)]
        send(rcopy(piece, coto.at[:, pl.ds(g * 384, 384)], es.at[g], er.at[g], core_p))

    def arrived(*numbers):
        @pl.when(m == 0)
        def _():
            for n in numbers:
                wait_on(cotb.at[:, parts[n][0]], cr.at[n])

    def partials(g):
        cols = pl.ds(g * 384, 384)
        wait_on(coto.at[:, cols], er.at[g])
        for r in range(2):
            rows = pl.ds(r * 640, 640)
            gbuf[g, rows, :] = dot(xts[c, rows, :], cotb[:, cols], ((1,), (0,))) + dot(
                xto[rows, :], coto[:, cols], ((1,), (0,))
            )

    def dest(o):
        return pl.multiple_of(lax.rem(z + nz + o, nz) * 160, 16)

    def span_of(d, k):
        return pl.ds(80 * d, 80) if k == 0 else pl.ds(0, 160)

    def ring(g, k):
        for d in range(2):
            o = (4 - k) if d == 0 else (k - 4)
            first = dest(o)
            own = 80 * d
            if k >= 1:
                wait_on(rbuf.at[d, g, k - 1, span_of(d, k - 1), :], rr.at[d, g, k - 1])
            if k == 0:
                sbuf[d, g, k, own : own + 80, :] = gbuf[g, pl.ds(first + own, 80), :].astype(BF16)
            elif k == 1:
                rest = 80 - own
                sbuf[d, g, k, own : own + 80, :] = (
                    gbuf[g, pl.ds(first + own, 80), :] + rbuf[d, g, 0, own : own + 80, :].astype(F32)
                ).astype(BF16)
                sbuf[d, g, k, rest : rest + 80, :] = gbuf[g, pl.ds(first + rest, 80), :].astype(BF16)
            else:
                sbuf[d, g, k, :, :] = (
                    gbuf[g, pl.ds(first, 160), :] + rbuf[d, g, k - 1, :, :].astype(F32)
                ).astype(BF16)
        for d in range(2):
            piece = sbuf.at[d, g, k, span_of(d, k), :]
            send(
                rcopy(
                    piece, rbuf.at[d, g, k, span_of(d, k), :],
                    rs.at[d, g, k], rr.at[d, g, k], up_z if d == 0 else dn_z,
                )
            )

    def finish(g):
        for d in range(2):
            wait_on(rbuf.at[d, g, 3], rr.at[d, g, 3])
        fbuf[g] = (
            gbuf[g, pl.ds(dest(0), 160), :]
            + (rbuf[0, g, 3].astype(F32) + rbuf[1, g, 3].astype(F32))
        ).astype(BF16)

    final_parts = ((1, 0, 256, False), (1, 256, 128, True), (2, 0, 384, True), (0, 0, 384, False))

    def deliver(g):
        for n, (pg, lo, width, crossed) in enumerate(final_parts):
            if pg != g:
                continue
            piece = fbuf.at[g, :, pl.ds(lo, width)]
            dst = obuf.at[g, :, pl.ds(lo, width)]
            straight = jnp.logical_or(m == 1, not crossed)
            send(rcopy(piece, dst, fs.at[n, 0], fr.at[n], turn), jnp.logical_and(straight, away))

            @pl.when(jnp.logical_and(straight, home))
            def _():
                pltpu.make_async_copy(piece, dst, fr.at[n]).start()

            if crossed:
                send(rcopy(piece, dst, fs.at[n, 1], fr.at[n], at(c=1 - yh, yh=c)), m == 0)

    def direction():
        for dm in range(2):
            for dx in range(4):
                for b in range(2):
                    wait_on(
                        dbuf.at[lax.rem(m + dm, 2), :, pl.ds(pl.multiple_of((lax.rem(x + nx - dx, nx) * 2 + b) * 384, 128), 384)],
                        dr.at[dm, dx, b],
                    )
        dir_ref[...] = (dbuf[1].astype(F32) - dbuf[0].astype(F32)).astype(BF16)

    for q in range(4):
        wait_on(xto.at[pl.ds(q * 320, 320), :], xtr.at[q])
    arrived(0, 1)
    exchange(1)
    partials(1)
    ring(1, 0)
    arrived(2)
    exchange(2)
    partials(2)
    ring(1, 1)
    ring(2, 0)
    arrived(3)
    exchange(0)
    partials(0)
    ring(1, 2)
    ring(2, 1)
    ring(0, 0)
    direction()
    ring(1, 3)
    ring(2, 2)
    ring(0, 1)
    finish(1)
    deliver(1)
    ring(2, 3)
    ring(0, 2)
    finish(2)
    deliver(2)
    ring(0, 3)
    finish(0)
    deliver(0)
    for n, (g, lo, width, crossed) in enumerate(final_parts):
        wait_on(obuf.at[g, :, pl.ds(lo, width)], fr.at[n])
    grad_ref[...] = obuf[...]
    for cp, cond in pending:
        if cond is None:
            cp.wait_send()
        else:
            pl.when(cond)(cp.wait_send)


def per_device(latents, noise, noise_level, group_index, projections, upstream):
    weights = jnp.transpose(projections[0], (1, 0, 2))
    groups = jnp.broadcast_to(group_index, (8, group_index.shape[1]))
    dma = pltpu.SemaphoreType.DMA
    vmem = pltpu.VMEM
    anywhere = pl.BlockSpec(memory_space=pl.ANY)
    direction, grads = pl.pallas_call(
        step_kernel,
        out_shape=(
            jax.ShapeDtypeStruct((32, 3072), BF16),
            jax.ShapeDtypeStruct((3, 160, 384), BF16),
        ),
        in_specs=[anywhere, anywhere, pl.BlockSpec(memory_space=pltpu.SMEM), anywhere, anywhere, anywhere],
        out_specs=(pl.BlockSpec(memory_space=pltpu.VMEM), pl.BlockSpec(memory_space=pltpu.VMEM)),
        scratch_shapes=[
            vmem((8, 640, 1152), BF16),
            vmem((8, 512, 640), BF16),
            vmem((8, 256, 640), BF16),
            vmem((8, 256, 640), BF16),
            vmem((512, 1152), F32),
            vmem((512, 1152), BF16),
            vmem((512, 384), BF16),
            vmem((8, 512), jnp.int32),
            vmem((512, 128), jnp.int32),
            vmem((512, 384), BF16),
            vmem((512, 1152), BF16),
            vmem((512, 1152), BF16),
            vmem((2, 1280, 512), BF16),
            vmem((1280, 512), BF16),
            vmem((512, 512), BF16),
            vmem((512, 512), BF16),
            vmem((3, 1280, 384), F32),
            vmem((2, 3, 4, 160, 384), BF16),
            vmem((2, 3, 4, 160, 384), BF16),
            vmem((3, 160, 384), BF16),
            vmem((3, 160, 384), BF16),
            vmem((2, 32, 3072), BF16),
            dma((8, 2)), dma((8, 2)), dma((2, 8, 2)), dma((8, 2)), dma((2, 3)),
            dma((3, 8)), dma((3, 8)), dma((8, 2)), dma((4,)), dma((4,)), dma((4,)),
            dma((4,)), dma((4,)), dma((3,)), dma((3,)),
            dma((2, 3, 4)), dma((2, 3, 4)), dma((4,)), dma((4, 2)),
            dma((2, 4, 2)), dma((2, 4, 2)),
        ],
        compiler_params=pltpu.CompilerParams(
            collective_id=0, has_side_effects=True, vmem_limit_bytes=62 << 20
        ),
    )(latents[0], noise[0], noise_level, weights, upstream[0], groups)
    grads = jnp.transpose(grads.astype(F32), (1, 0, 2))
    return direction[None], grads


def solution(mesh):
    split = Mesh(
        mesh.devices.reshape(2, mesh.shape["seq"] // 2, 2, mesh.shape["fsdp"] // 2, 2), AXES
    )
    clip, heads = ("z", "yh"), ("x", "c")
    return jax.shard_map(
        step_kernel_call,
        mesh=split,
        in_specs=(
            P(clip, "m", None),
            P(clip, "m", None),
            P(clip),
            P(clip, None),
            P("m", clip, None, heads),
            P(clip, None, heads),
        ),
        out_specs=(P(clip, ("m", "x", "c"), None), P(("m", "z", "yh"), None, heads)),
        check_vma=False,
    )


step_kernel_call = per_device
```

time: 508 us -> 154 us (0.30)
  waiting for transfers between devices: 398 us -> 0 us
  Pallas kernels: 0 us -> 148 us
  matrix products: 36.5 us -> 0 us
  blocking collectives: 20.2 us -> 0 us
  local copies, waits for them, and re-layouts: 19.6 us -> 2.9 us
  other arithmetic: 17.1 us -> 1.9 us
  between operations: 14.6 us -> 1.29 us
    all_gather x2 -> x0, waiting for transfers between devices: 301 us -> none  [the longest x1 164 us: per_device(): weight_piece = lax.all_gather(projections, FSDP, axis=1, tiled=True)]
    pallas_call x0 -> x1, Pallas kernels: none -> 148 us  [per_device(): pl.pallas_call(step_kernel, out_shape=(jax.ShapeDtypeStruct((32, 3072), B...]
    reduce_scatter x2 -> x0, waiting for transfers between devices: 70 us -> none  [summed_rows(): total = lax.psum_scatter(total, axis, scatter_dimension=0, tiled=True)]
    dot_general x8 -> x0, matrix products: 36.5 us -> none  [the longest x1 10.8 us: per_device(): jnp.dot(columns, weight_piece.reshape(row_count, triple_width), preferred...]
    ppermute x1 -> x0, waiting for transfers between devices: 26.5 us -> none  [shifted(): return lax.ppermute(value, axis, pairs)]
    all_to_all x2 -> x0, blocking collectives: 20.2 us -> none  [the longest x1 12.1 us: per_device(): lax.all_to_all(paired.astype(jnp.bfloat16), 'seq', split_axis=0, concat_a...]
    all_gather x1 -> x0, local copies, waits for them, and re-layouts: 15 us -> none  [per_device(): weight_piece = lax.all_gather(projections, FSDP, axis=1, tiled=True)]
    convert_element_type x1 -> x0, other arithmetic: 8.55 us -> none  [per_device(): noised = ((1.0 - noise_rate) * clip_rows.astype(jnp.float32) + noise_rate...]
  transfers between devices with their start and end apart: 5 -> 0, of which waited for: 5 -> 0; matrix products, arithmetic and copies ran while one was open for 2% -> 0% of each run, Pallas kernels for 0% -> 0%
where the time goes in v1:
time: 154 us
  Pallas kernels  148 us (96%)
  local copies, waits for them, and re-layouts  2.9 us (2%)
  other arithmetic  1.9 us (1%)
    pallas_call x1, Pallas kernels, per_device(): pl.pallas_call(step_kernel, out_shape=(jax.ShapeDtypeStruct((32, 3072), B...  148 us

profile of v1, /device:TPU:1, one launch (start us, length us, event | category | flops | bytes accessed | tf_op | source)
XLA Modules:
  0.0 154.0 jit_solution(1785352732739146017)
XLA Ops:
  1.3 1.3 broadcast_in_dim.11.gi_ref
  2.6 147.9 %shard_map.77 = (bf16[32,3072]{1,0:T(8,128)(2,1)}, bf16[3,160,384]{2,1,0:T(8,128)(2,1)}) custom-call(bf16[256,5120]{1,0:T(8,128)(2,1)} %bitcast.10, bf16[256,5120]{1,0:T(8,128)(2,1)} %bitcast.11, f32[1]{0:T(128)S(6)} %copy.9.lvl_ref, bf16[3,320,384]{2,1,0:T(8,128)(2,1)} %bitcast.12, bf16[512,384]{1,0:T(8,128)(2,1)} %bitcast.13, s32[8,512]{1,0:T(8,128)} %broadcast_in_dim.11.gi_ref), custom_call_target="tpu_custom_call" | custom-call | tf_op jit(solution)/shard_map/pallas_call | solution.py:476
  150.5 1.9 %convert_bitcast_fusion = f32[160,3,384]{2,0,1:T(8,128)} fusion(bf16[3,160,384]{2,1,0:T(8,128)(2,1)} %get-tuple-element.5), kind=kLoop, calls=%fused_computation | loop fusion | flops 184320 | bytes 1105920 | tf_op jit(solution)/shard_map/transpose | solution.py:517
  152.4 1.6 %copy.10 = bf16[1,32,3072]{2,1,0:T(8,128)(2,1)} copy(bf16[1,32,3072]{2,1,0:T(8,128)(2,1)} %bitcast.14) | data formatting | bytes 393216

commit v2 on v1

--- a/solution.py
+++ b/solution.py
@@ -14,7 +14,6 @@
 F32 = jnp.float32
 BF16 = jnp.bfloat16
 OFFSETS = (0, -1, 1, -2, 2, -3, 3, 4)
-GROUP_ORDER = (1, 2, 0)
 
 
 def dot(a, b, dims):
@@ -277,8 +276,9 @@
     gcol[...] = jnp.transpose(jnp.broadcast_to(gib[0:1, :], (128, 512)))
     scale = 1.0 / math.sqrt(HEAD)
     fake = m == 1
-    for h in range(3):
+    def attend(h):
         qc, kc, vc = (pl.ds(j * 384 + h * 128, 128) for j in range(3))
+        dq, dk, dv = (pl.ds(h * 384 + j * 128, 128) for j in range(3))
         hc = pl.ds(h * 128, 128)
         for b in range(4):
             nk = min(512, (b + 2) * 128)
@@ -297,7 +297,7 @@
                 dp = dot(upb[rows, hc], tri[0:nk, vc], ((1,), (1,)))
                 inner = jnp.sum(p * dp, axis=-1, keepdims=True)
                 ds = (p * (dp - inner) * scale).astype(BF16)
-                cotb[rows, qc] = dot(ds, tri[0:nk, kc], ((1,), (0,))).astype(BF16)
+                cotb[rows, dq] = dot(ds, tri[0:nk, kc], ((1,), (0,))).astype(BF16)
                 pbuf[rows, 0:nk] = low
                 dsbuf[rows, 0:nk] = ds
 
@@ -307,22 +307,23 @@
                 first = max(0, (b - 1) * 128)
                 rows = pl.ds(first, 512 - first)
                 keys = pl.ds(b * 128, 128)
-                cotb[keys, vc] = dot(pbuf[rows, keys], upb[rows, hc], ((0,), (0,))).astype(BF16)
-                cotb[keys, kc] = dot(dsbuf[rows, keys], tri[rows, qc], ((0,), (0,))).astype(BF16)
-
-    parts = (
-        (pl.ds(384, 256), sib),
-        (pl.ds(640, 128), out),
-        (pl.ds(768, 384), out),
-        (pl.ds(0, 384), sib),
-    )
-    for n, (cols, peer) in enumerate(parts):
-        piece = cotb.at[:, cols]
-        send(rcopy(piece, piece, cs.at[n], cr.at[n], peer), fake)
+                cotb[keys, dv] = dot(pbuf[rows, keys], upb[rows, hc], ((0,), (0,))).astype(BF16)
+                cotb[keys, dk] = dot(dsbuf[rows, keys], tri[rows, qc], ((0,), (0,))).astype(BF16)
+
+    split_at = (256, 128, 256)
+
+    def part(g, n):
+        lo, hi = ((0, split_at[g]), (split_at[g], 384))[n]
+        return pl.ds(g * 384 + lo, hi - lo)
+
+    def spread(g):
+        for n, peer in ((0, sib), (1, out)):
+            piece = cotb.at[:, part(g, n)]
+            send(rcopy(piece, piece, cs.at[g, n], cr.at[g, n], peer), fake)
 
     mine_cols = pl.ds(pl.multiple_of((x * 2 + yh) * 384, 128), 384)
-    for dm in range(2):
-        for dx in range(4):
+
+    def direction_send(dm, dx):
             for dc in range(2):
                 tm, tx, tc = lax.rem(m + dm, 2), lax.rem(x + dx, nx), lax.rem(c + dc, 2)
                 src = attb.at[pl.ds(pl.multiple_of((tm * 8 + tx * 2 + tc) * 32, 32), 32), :]
@@ -338,15 +339,15 @@
                 else:
                     send(cp)
 
-    def exchange(g):
+    def exchange(g, cond):
         piece = cotb.at[:, pl.ds(g * 384, 384)]
-        send(rcopy(piece, coto.at[:, pl.ds(g * 384, 384)], es.at[g], er.at[g], core_p))
-
-    def arrived(*numbers):
+        send(rcopy(piece, coto.at[:, pl.ds(g * 384, 384)], es.at[g], er.at[g], core_p), cond)
+
+    def arrived(g):
         @pl.when(m == 0)
         def _():
-            for n in numbers:
-                wait_on(cotb.at[:, parts[n][0]], cr.at[n])
+            for n in range(2):
+                wait_on(cotb.at[:, part(g, n)], cr.at[g, n])
 
     def partials(g):
         cols = pl.ds(g * 384, 384)
@@ -399,23 +400,19 @@
             + (rbuf[0, g, 3].astype(F32) + rbuf[1, g, 3].astype(F32))
         ).astype(BF16)
 
-    final_parts = ((1, 0, 256, False), (1, 256, 128, True), (2, 0, 384, True), (0, 0, 384, False))
-
     def deliver(g):
-        for n, (pg, lo, width, crossed) in enumerate(final_parts):
-            if pg != g:
-                continue
-            piece = fbuf.at[g, :, pl.ds(lo, width)]
-            dst = obuf.at[g, :, pl.ds(lo, width)]
-            straight = jnp.logical_or(m == 1, not crossed)
-            send(rcopy(piece, dst, fs.at[n, 0], fr.at[n], turn), jnp.logical_and(straight, away))
+        for n, (lo, hi) in enumerate(((0, split_at[g]), (split_at[g], 384))):
+            piece = fbuf.at[g, :, pl.ds(lo, hi - lo)]
+            dst = obuf.at[g, :, pl.ds(lo, hi - lo)]
+            straight = jnp.logical_or(m == 1, n == 0)
+            send(rcopy(piece, dst, fs.at[g, n, 0], fr.at[g, n], turn), jnp.logical_and(straight, away))
 
             @pl.when(jnp.logical_and(straight, home))
             def _():
-                pltpu.make_async_copy(piece, dst, fr.at[n]).start()
-
-            if crossed:
-                send(rcopy(piece, dst, fs.at[n, 1], fr.at[n], at(c=1 - yh, yh=c)), m == 0)
+                pltpu.make_async_copy(piece, dst, fr.at[g, n]).start()
+
+            if n == 1:
+                send(rcopy(piece, dst, fs.at[g, n, 1], fr.at[g, n], at(c=1 - yh, yh=c)), m == 0)
 
     def direction():
         for dm in range(2):
@@ -427,39 +424,55 @@
                     )
         dir_ref[...] = (dbuf[1].astype(F32) - dbuf[0].astype(F32)).astype(BF16)
 
+    def shared(g):
+        arrived(g)
+        exchange(g, m == 0)
+
+    attend(0)
+    spread(0)
+    exchange(0, fake)
+    attend(1)
+    spread(1)
+    exchange(1, fake)
     for q in range(4):
         wait_on(xto.at[pl.ds(q * 320, 320), :], xtr.at[q])
-    arrived(0, 1)
-    exchange(1)
+    shared(0)
+    partials(0)
+    ring(0, 0)
+    attend(2)
+    spread(2)
+    exchange(2, fake)
+    shared(1)
     partials(1)
+    ring(0, 1)
     ring(1, 0)
-    arrived(2)
-    exchange(2)
+    for dm in range(2):
+        for dx in range(4):
+            direction_send(dm, dx)
+    shared(2)
     partials(2)
+    ring(0, 2)
     ring(1, 1)
     ring(2, 0)
-    arrived(3)
-    exchange(0)
-    partials(0)
+    ring(0, 3)
     ring(1, 2)
     ring(2, 1)
-    ring(0, 0)
-    direction()
+    finish(0)
+    deliver(0)
     ring(1, 3)
     ring(2, 2)
-    ring(0, 1)
     finish(1)
     deliver(1)
     ring(2, 3)
-    ring(0, 2)
+    direction()
     finish(2)
     deliver(2)
-    ring(0, 3)
-    finish(0)
-    deliver(0)
-    for n, (g, lo, width, crossed) in enumerate(final_parts):
-        wait_on(obuf.at[g, :, pl.ds(lo, width)], fr.at[n])
-    grad_ref[...] = obuf[...]
+    for g in range(3):
+        for n in range(2):
+            lo, hi = ((0, split_at[g]), (split_at[g], 384))[n]
+            wait_on(obuf.at[g, :, pl.ds(lo, hi - lo)], fr.at[g, n])
+        for j in range(3):
+            grad_ref[j, :, pl.ds(g * 128, 128)] = obuf[g, :, pl.ds(j * 128, 128)]
     for cp, cond in pending:
         if cond is None:
             cp.wait_send()
@@ -506,8 +519,8 @@
             vmem((2, 32, 3072), BF16),
             dma((8, 2)), dma((8, 2)), dma((2, 8, 2)), dma((8, 2)), dma((2, 3)),
             dma((3, 8)), dma((3, 8)), dma((8, 2)), dma((4,)), dma((4,)), dma((4,)),
-            dma((4,)), dma((4,)), dma((3,)), dma((3,)),
-            dma((2, 3, 4)), dma((2, 3, 4)), dma((4,)), dma((4, 2)),
+            dma((3, 2)), dma((3, 2)), dma((3,)), dma((3,)),
+            dma((2, 3, 4)), dma((2, 3, 4)), dma((3, 2)), dma((3, 2, 2)),
             dma((2, 4, 2)), dma((2, 4, 2)),
         ],
         compiler_params=pltpu.CompilerParams(

time: 154 us -> 145 us (0.942)
  Pallas kernels: 148 us -> 139 us
    pallas_call x1, Pallas kernels: 148 us -> 139 us  [per_device(): pl.pallas_call(step_kernel, out_shape=(jax.ShapeDtypeStruct((32, 3072), B...]
where the time goes in v2:
time: 145 us
  Pallas kernels  139 us (96%)
  local copies, waits for them, and re-layouts  2.9 us (2%)
  other arithmetic  1.9 us (1%)
    pallas_call x1, Pallas kernels, per_device(): pl.pallas_call(step_kernel, out_shape=(jax.ShapeDtypeStruct((32, 3072), B...  139 us

profile of v2, /device:TPU:1, one launch (start us, length us, event | category | flops | bytes accessed | tf_op | source)
XLA Modules:
  0.0 144.7 jit_solution(11612224495947158238)
XLA Ops:
  1.3 1.3 broadcast_in_dim.11.gi_ref
  2.6 138.6 %shard_map.77 = (bf16[32,3072]{1,0:T(8,128)(2,1)}, bf16[3,160,384]{2,1,0:T(8,128)(2,1)}) custom-call(bf16[256,5120]{1,0:T(8,128)(2,1)} %bitcast.10, bf16[256,5120]{1,0:T(8,128)(2,1)} %bitcast.11, f32[1]{0:T(128)S(6)} %copy.9.lvl_ref, bf16[3,320,384]{2,1,0:T(8,128)(2,1)} %bitcast.12, bf16[512,384]{1,0:T(8,128)(2,1)} %bitcast.13, s32[8,512]{1,0:T(8,128)} %broadcast_in_dim.11.gi_ref), custom_call_target="tpu_custom_call" | custom-call | tf_op jit(solution)/shard_map/pallas_call | solution.py:489
  141.2 1.9 %convert_bitcast_fusion = f32[160,3,384]{2,0,1:T(8,128)} fusion(bf16[3,160,384]{2,1,0:T(8,128)(2,1)} %get-tuple-element.5), kind=kLoop, calls=%fused_computation | loop fusion | flops 184320 | bytes 1105920 | tf_op jit(solution)/shard_map/transpose | solution.py:530
  143.1 1.6 %copy.10 = bf16[1,32,3072]{2,1,0:T(8,128)(2,1)} copy(bf16[1,32,3072]{2,1,0:T(8,128)(2,1)} %bitcast.14) | data formatting | bytes 393216

commit v3 on v2

v3 whole, which is shorter than its diff:
```python
import math

import jax
import jax.numpy as jnp
from jax import lax
from jax.experimental import pallas as pl
from jax.experimental.pallas import tpu as pltpu
from jax.sharding import Mesh
from jax.sharding import PartitionSpec as P

HEAD = 128
AXES = ("m", "x", "c", "z", "yh")
MESH_ID = pl.DeviceIdType.MESH
F32 = jnp.float32
BF16 = jnp.bfloat16
OFFSETS = (0, -1, 1, -2, 2, -3, 3, 4)


def dot(a, b, dims):
    return lax.dot_general(a, b, (dims, ((), ())), preferred_element_type=F32)


def step_kernel(
    lat_ref, noi_ref, lvl_ref, proj_ref, up_ref, gi_ref,
    dir_ref, grad_ref,
    wbuf, xbuf, latv, noiv, acc, tri, upb, gib, gcol, attb, cotb, coto,
    xts, xto, pbuf, dsbuf, gbuf, sbuf, rbuf, fbuf, obuf, dbuf,
    wr, wc, ws, wcs, wos, ya, xa, xs, xxs, lsem, usem, xtr, xtss, cr, cs, er, es,
    rr, rs, fr, fs, dr, dsm,
):
    m, x, c, z, yh = (lax.axis_index(a) for a in AXES)
    nz = lax.axis_size("z")
    nx = lax.axis_size("x")
    home = c == yh
    away = c != yh

    def at(**k):
        return k

    core_p = at(c=1 - c)
    sib = at(m=1 - m)
    out = at(m=1 - m, yh=1 - yh)
    turn = at(c=yh, yh=c)
    up_z = at(z=lax.rem(z + 1, nz))
    dn_z = at(z=lax.rem(z + nz - 1, nz))
    blk = [lax.rem(z + nz + o, nz) for o in OFFSETS]

    def rcopy(src, dst, ss, rsem, dev):
        return pltpu.make_async_remote_copy(
            src_ref=src, dst_ref=dst, send_sem=ss, recv_sem=rsem,
            device_id=dev, device_id_type=MESH_ID,
        )

    def wait_on(ref, sem):
        pltpu.make_async_copy(ref, ref, sem).wait()

    pending = []

    def go(cp, cond=None):
        if cond is None:
            cp.start()
        else:
            pl.when(cond)(cp.start)

    def send(cp, cond=None):
        go(cp, cond)
        pending.append((cp.wait_send, cond))

    def sent(ref, sem, cond=None):
        pending.append((lambda: wait_on(ref, sem), cond))

    def settle(number):
        for wait, cond in pending[:number]:
            if cond is None:
                wait()
            else:
                pl.when(cond)(wait)
        del pending[:number]

    rows_m = pl.ds(pl.multiple_of(m * 256, 256), 256)

    def read(p, which):
        src, dst = ((lat_ref, latv), (noi_ref, noiv))[which]
        return pltpu.make_async_copy(src.at[:, pl.ds(p * 1280, 1280)], dst.at[p], lsem.at[p, which])

    def w_rows(zb, core, i):
        return pl.ds(pl.multiple_of(zb * 640 + core * 320 + i * 160, 16), 160)

    def own_rows(h, i, j):
        return (
            proj_ref.at[j, pl.ds(160 * i, 160), pl.ds(128 * h, 128)],
            wbuf.at[h, w_rows(z, yh, i), pl.ds(128 * j, 128)],
        )

    every_own = [(h, i, j) for h in range(3) for i in range(2) for j in range(3)]

    @pl.when(home)
    def _():
        for h, i, j in every_own:
            pltpu.make_async_copy(*own_rows(h, i, j), wr.at[h, 0, i]).start()
            if (i, j) == (1, 2) and h < 2:
                for p in (2 * h, 2 * h + 1):
                    read(p, 0).start()
                    read(p, 1).start()

    barrier = pltpu.get_barrier_semaphore()
    count = 0
    for dm in range(2):
        for dx in range(4):
            for dc in range(2):
                for dy in range(2):
                    if dm + dx + dc + dy == 0:
                        continue
                    peer = at(
                        m=lax.rem(m + dm, 2), x=lax.rem(x + dx, nx),
                        c=lax.rem(c + dc, 2), yh=lax.rem(yh + dy, 2),
                    )
                    pl.semaphore_signal(barrier, inc=1, device_id=peer, device_id_type=MESH_ID)
                    count += 1
    for peer in (up_z, dn_z):
        pl.semaphore_signal(barrier, inc=1, device_id=peer, device_id_type=MESH_ID)
        count += 1
    pl.semaphore_wait(barrier, count)

    def w_turn(h):
        for i in range(2):
            for j in range(3):
                src, dst = own_rows(h, i, j)
                go(rcopy(src, dst, wos.at[h], wr.at[h, 0, i], turn), away)
        sent(wbuf.at[h, 0:320, :], wos.at[h], away)

    w_turn(0)

    def side_inputs():
        send(rcopy(gi_ref, gib, usem.at[2], usem.at[3], turn), away)
        send(rcopy(up_ref, upb, usem.at[0], usem.at[1], turn), jnp.logical_and(away, m == 1))

        @pl.when(jnp.logical_or(home, m == 0))
        def _():
            pltpu.make_async_copy(up_ref, upb, usem.at[1]).start()

        @pl.when(home)
        def _():
            pltpu.make_async_copy(gi_ref, gib, usem.at[3]).start()

    rate = lvl_ref[0]

    up_x = at(x=lax.rem(x + 1, nx))
    dn_x = at(x=lax.rem(x + nx - 1, nx))

    def quarter(half, step):
        first = half * 256 + lax.rem(x + nx + step, nx) * 64
        return pl.ds(pl.multiple_of(first, 64), 64)

    def noise(p):
        @pl.when(home)
        def _():
            read(p, 0).wait()
            read(p, 1).wait()
            for lo in (0, 640):
                xbuf[p, rows_m, lo : lo + 640] = (
                    (1.0 - rate) * latv[p, :, lo : lo + 640].astype(F32)
                    + rate * noiv[p, :, lo : lo + 640].astype(F32)
                ).astype(BF16)

    def x_own(p):
        for q in range(2):
            piece = xbuf.at[p, quarter(m, q), :]
            go(rcopy(piece, piece, xs.at[p], ya.at[p, 0], sib), home)
            go(rcopy(piece, piece, xs.at[p], ya.at[p, 0], out), home)

    def x_side(p, kind, q, cond):
        piece = xbuf.at[p, quarter((1 - m) if kind == 0 else m, q), :]
        go(rcopy(piece, piece, xxs.at[p], xa.at[p, kind], up_x if q == 0 else dn_x), cond)

    def x_y(p):
        wait_on(xbuf.at[p, 0:128, :], ya.at[p, 0])
        for q in range(2):
            piece = xbuf.at[p, quarter(1 - m, q), :]
            if p % 2 == 1:
                go(rcopy(piece, piece, xs.at[p], ya.at[p, 1], out), home)
            else:
                go(rcopy(piece, piece, xs.at[p], ya.at[p, 1], sib), away)
            x_side(p, 0, q, None)

    def x_z(p):
        @pl.when(away)
        def _():
            wait_on(xbuf.at[p, 0:128, :], ya.at[p, 1])

        for q in range(2):
            x_side(p, 1, q, away)

    def x_ready(p):
        wait_on(xbuf.at[p, 0:128, :], xa.at[p, 0])

        @pl.when(away)
        def _():
            wait_on(xbuf.at[p, 0:128, :], xa.at[p, 1])

        sent(xbuf.at[p, 0 : 256 + 128 * (p % 2), :], xs.at[p], home)
        if p % 2 == 0:
            sent(xbuf.at[p, 0:128, :], xs.at[p], away)
        sent(xbuf.at[p, 0:128, :], xxs.at[p], home)
        sent(xbuf.at[p, 0:256, :], xxs.at[p], away)

    def w_event(h, k, i, cond=None):
        piece = wbuf.at[h, w_rows(blk[k], c, i), :]
        if cond is None:
            wait_on(piece, wr.at[h, k, i])
        else:
            pl.when(cond)(lambda: wait_on(piece, wr.at[h, k, i]))
        o = OFFSETS[k]
        if -3 < o <= 0 or (o == -3 and i == 0):
            to = OFFSETS.index(o - 1 if o > -3 else 4)
            go(rcopy(piece, piece, ws.at[h], wr.at[h, to, i], up_z), cond)
        if 0 <= o < 3 or (o == 3 and i == 1):
            go(rcopy(piece, piece, ws.at[h], wr.at[h, OFFSETS.index(o + 1), i], dn_z), cond)
        go(rcopy(piece, piece, wcs.at[h], wc.at[h, k], core_p), cond)

    def stage(h, n, i):
        w_event(h, 2 * n - 1, i)
        w_event(h, 2 * n, i)

    def last(h):
        w_event(h, 7, 0)
        w_event(h, 7, 1)
        sent(wbuf.at[h, 0:2240, :], ws.at[h])
        sent(wbuf.at[h, 0:2560, :], wcs.at[h])

    def w_other(h, k):
        first = pl.multiple_of(blk[k] * 640 + (1 - c) * 320, 64)
        wait_on(wbuf.at[h, pl.ds(first, 320), :], wc.at[h, k])

    def gather(first, part):
        if first:
            acc[...] = part
        else:
            acc[...] += part

    def multiply_columns(p):
        if p == 0:
            for k in range(8):
                w_other(0, k)
        gather(p == 0, dot(xbuf[p], wbuf[0, p * 1280 : (p + 1) * 1280, :], ((1,), (0,))))

    def multiply(h, *blocks):
        for k in blocks:
            w_other(h, k)
            cols = pl.ds(pl.multiple_of(lax.rem(blk[k], 2) * 640, 128), 640)
            rows = pl.ds(pl.multiple_of(blk[k] * 640, 128), 640)
            gather(k == 0, dot(xbuf[blk[k] // 2, :, cols], wbuf[h, rows, :], ((1,), (0,))))

    def keep(h):
        tri[h] = acc[...].astype(BF16)

    def turned(p):
        @pl.when(m == p // 2)
        def _():
            base = (p % 2) * 640
            for i in range(10):
                t = xbuf[p, :, i * 128 : (i + 1) * 128].T
                r = i * 128
                while r < (i + 1) * 128:
                    end = min((i + 1) * 128, (r // 160 + 1) * 160)
                    first = base + (r // 320) * 160 + r % 160
                    xts[(r % 320) // 160, pl.ds(first, end - r), :] = t[r - i * 128 : end - i * 128, :]
                    r = end

    def turned_send(p):
        span = pl.ds((p % 2) * 640, 640)
        send(
            rcopy(xts.at[1 - c, span, :], xto.at[span, :], xtss.at[p % 2], xtr.at[p % 2], core_p),
            m == p // 2,
        )

    def attention_inputs():
        wait_on(gib, usem.at[3])
        wait_on(upb, usem.at[1])
        gcol[...] = jnp.transpose(jnp.broadcast_to(gib[...], (128, 512)))

    scale = 1.0 / math.sqrt(HEAD)
    fake = m == 1
    def attend(h):
        qc, kc, vc = (pl.ds(j * 128, 128) for j in range(3))
        dq = pl.ds(h * 384, 128)
        hc = pl.ds(h * 128, 128)
        for b in range(4):
            nk = min(512, (b + 2) * 128)
            rows = pl.ds(b * 128, 128)
            s = dot(tri[h, rows, qc], tri[h, 0:nk, kc], ((1,), (1,))) * scale
            mine = gcol[rows, :]
            visible = gib[0:1, 0:nk] <= jnp.concatenate([mine] * (nk // 128), axis=1)
            s = jnp.where(visible, s, F32(-1e30))
            w = jnp.exp(s - jnp.max(s, axis=-1, keepdims=True))
            p = w * (1.0 / jnp.sum(w, axis=-1, keepdims=True))
            low = p.astype(BF16)
            attb[rows, hc] = dot(low, tri[h, 0:nk, vc], ((1,), (0,))).astype(BF16)

            @pl.when(fake)
            def _():
                dp = dot(upb[rows, hc], tri[h, 0:nk, vc], ((1,), (1,)))
                inner = jnp.sum(p * dp, axis=-1, keepdims=True)
                ds = (p * (dp - inner) * scale).astype(BF16)
                cotb[rows, dq] = dot(ds, tri[h, 0:nk, kc], ((1,), (0,))).astype(BF16)
                pbuf[rows, 0:nk] = low
                dsbuf[rows, 0:nk] = ds

    def key_side(h, j):
        left, right = (
            (dsbuf, tri.at[h, :, pl.ds(0, 128)]) if j == 1 else (pbuf, upb.at[:, pl.ds(h * 128, 128)])
        )

        @pl.when(fake)
        def _():
            for b in range(4):
                first = max(0, (b - 1) * 128)
                rows = pl.ds(first, 512 - first)
                keys = pl.ds(b * 128, 128)
                cotb[keys, pl.ds(h * 384 + j * 128, 128)] = dot(
                    left[rows, keys], right[rows, :], ((0,), (0,))
                ).astype(BF16)

    parts = (
        (0, 0, 256, False), (0, 256, 128, True),
        (1, 384, 128, False), (1, 512, 256, True),
        (2, 768, 256, False),
        (3, 1024, 128, True),
    )
    groups = ((0, 384), (384, 384), (768, 256), (1024, 128))

    def spread(g):
        for n, (pg, col, width, outer) in enumerate(parts):
            if pg == g:
                piece = cotb.at[:, pl.ds(col, width)]
                send(rcopy(piece, piece, cs.at[n], cr.at[n], out if outer else sib), fake)

    mine_cols = pl.ds(pl.multiple_of((x * 2 + yh) * 384, 128), 384)

    def direction_send():
        for dm in range(2):
            for dx in range(4):
                for dc in range(2):
                    tm, tx, tc = lax.rem(m + dm, 2), lax.rem(x + dx, nx), lax.rem(c + dc, 2)
                    src = attb.at[pl.ds(pl.multiple_of((tm * 8 + tx * 2 + tc) * 32, 32), 32), :]
                    dst = dbuf.at[m, :, mine_cols]
                    sem = dr.at[dm, dx, yh]
                    cp = rcopy(src, dst, dsm, sem, at(m=tm, x=tx, c=tc, yh=c))
                    if dm + dx + dc == 0:
                        go(cp, away)

                        @pl.when(home)
                        def _():
                            pltpu.make_async_copy(src, dst, sem).start()
                    else:
                        go(cp)
        sent(attb.at[0:480, :], dsm, home)
        sent(attb, dsm, away)

    def exchange(g, cond):
        cols = pl.ds(*groups[g])
        send(rcopy(cotb.at[:, cols], coto.at[:, cols], es.at[g], er.at[g], core_p), cond)

    def arrived(g):
        @pl.when(m == 0)
        def _():
            for n, (pg, col, width, _) in enumerate(parts):
                if pg == g:
                    wait_on(cotb.at[:, pl.ds(col, width)], cr.at[n])

    def partials(g):
        cols = pl.ds(*groups[g])
        wait_on(coto.at[:, cols], er.at[g])
        for r in range(2):
            rows = pl.ds(r * 640, 640)
            gbuf[rows, cols] = dot(xts[c, rows, :], cotb[:, cols], ((1,), (0,))) + dot(
                xto[rows, :], coto[:, cols], ((1,), (0,))
            )

    def dest(o):
        return pl.multiple_of(lax.rem(z + nz + o, nz) * 160, 16)

    def span_of(d, k):
        return pl.ds(80 * d, 80) if k == 0 else pl.ds(0, 160)

    def ring(g, k):
        cols = pl.ds(*groups[g])
        for d in range(2):
            o = (4 - k) if d == 0 else (k - 4)
            first = dest(o)
            own, rest = pl.ds(80 * d, 80), pl.ds(80 - 80 * d, 80)
            mine = gbuf[pl.ds(first + 80 * d, 80), cols]
            if k >= 1:
                wait_on(rbuf.at[d, k - 1, span_of(d, k - 1), cols], rr.at[d, g, k - 1])
            if k == 0:
                sbuf[d, k, own, cols] = mine.astype(BF16)
            elif k == 1:
                sbuf[d, k, own, cols] = (mine + rbuf[d, 0, own, cols].astype(F32)).astype(BF16)
                sbuf[d, k, rest, cols] = gbuf[pl.ds(first + 80 - 80 * d, 80), cols].astype(BF16)
            else:
                sbuf[d, k, :, cols] = (
                    gbuf[pl.ds(first, 160), cols] + rbuf[d, k - 1, :, cols].astype(F32)
                ).astype(BF16)
            piece = sbuf.at[d, k, span_of(d, k), cols]
            cp = rcopy(
                piece, rbuf.at[d, k, span_of(d, k), cols],
                rs.at[d, g, min(k, 1)], rr.at[d, g, k], up_z if d == 0 else dn_z,
            )
            if k == 0:
                send(cp)
            else:
                go(cp)
        if k == 3:
            for d in range(2):
                sent(sbuf.at[d, 1:4, :, cols], rs.at[d, g, 1])

    def finish(g):
        cols = pl.ds(*groups[g])
        for d in range(2):
            wait_on(rbuf.at[d, 3, :, cols], rr.at[d, g, 3])
        fbuf[:, cols] = (
            gbuf[pl.ds(dest(0), 160), cols]
            + (rbuf[0, 3, :, cols].astype(F32) + rbuf[1, 3, :, cols].astype(F32))
        ).astype(BF16)

    def deliver(g):
        for n, (pg, col, width, outer) in enumerate(parts):
            if pg != g:
                continue
            piece = fbuf.at[:, pl.ds(col, width)]
            dst = obuf.at[:, pl.ds(col, width)]
            straight = (m == 1) if outer else (m <= 1)
            send(rcopy(piece, dst, fs.at[n, 0], fr.at[n], turn), jnp.logical_and(straight, away))

            @pl.when(jnp.logical_and(straight, home))
            def _():
                pltpu.make_async_copy(piece, dst, fr.at[n]).start()

            if outer:
                send(rcopy(piece, dst, fs.at[n, 1], fr.at[n], at(c=1 - yh, yh=c)), m == 0)

    def received(g):
        for n, (pg, col, width, _) in enumerate(parts):
            if pg == g:
                wait_on(obuf.at[:, pl.ds(col, width)], fr.at[n])
                for k in range(width // 128):
                    p = col // 128 + k
                    grad_ref[p % 3, :, pl.ds(p // 3 * 128, 128)] = obuf[:, pl.ds(p * 128, 128)]

    def direction():
        for dm in range(2):
            for dx in range(4):
                for b in range(2):
                    wait_on(
                        dbuf.at[lax.rem(m + dm, 2), :, pl.ds(pl.multiple_of((lax.rem(x + nx - dx, nx) * 2 + b) * 384, 128), 384)],
                        dr.at[dm, dx, b],
                    )
        dir_ref[...] = (dbuf[1].astype(F32) - dbuf[0].astype(F32)).astype(BF16)

    def shared(g):
        arrived(g)
        exchange(g, m == 0)

    def launch(h):
        attend(h)
        key_side(h, 2)
        if h == 2:
            spread(3)
            exchange(3, fake)
        key_side(h, 1)
        spread(h)
        exchange(h, fake)

    noise(0)
    x_own(0)
    w_event(0, 0, 0, home)
    w_event(0, 0, 1, home)
    w_event(1, 0, 0, home)
    w_event(1, 0, 1, home)
    noise(1)
    x_own(1)
    w_event(0, 0, 0, away)
    w_event(0, 0, 1, away)
    w_turn(1)
    stage(0, 1, 0)
    x_y(0)
    w_event(2, 0, 0, home)
    noise(2)
    x_own(2)
    stage(0, 1, 1)
    w_event(2, 0, 1, home)
    x_y(1)
    stage(0, 2, 0)
    w_turn(2)
    w_event(1, 0, 0, away)
    x_z(0)
    noise(3)
    x_own(3)
    stage(0, 2, 1)
    w_event(1, 0, 1, away)
    x_y(2)
    stage(0, 3, 0)
    x_z(1)
    stage(0, 3, 1)
    side_inputs()
    x_ready(0)
    turned(0)
    last(0)
    stage(1, 1, 0)
    x_y(3)
    x_z(2)
    multiply_columns(0)
    turned_send(0)
    stage(1, 1, 1)
    x_z(3)
    x_ready(1)
    multiply_columns(1)
    turned(1)
    stage(1, 2, 0)
    w_event(2, 0, 0, away)
    x_ready(2)
    multiply_columns(2)
    turned(2)
    turned_send(1)
    stage(1, 2, 1)
    w_event(2, 0, 1, away)
    x_ready(3)
    multiply_columns(3)
    keep(0)
    stage(1, 3, 0)
    multiply(1, 0, 1)
    stage(1, 3, 1)
    attention_inputs()
    launch(0)
    turned(3)
    turned_send(2)
    turned_send(3)
    last(1)
    multiply(1, 2, 3, 4)
    stage(2, 1, 0)
    multiply(1, 5, 6, 7)
    keep(1)
    stage(2, 1, 1)
    launch(1)
    stage(2, 2, 0)
    multiply(2, 0)
    for q in range(2):
        wait_on(xto.at[pl.ds(q * 640, 640), :], xtr.at[q])
    shared(0)
    stage(2, 2, 1)
    multiply(2, 1, 2)
    partials(0)
    stage(2, 3, 0)
    multiply(2, 3, 4)
    stage(2, 3, 1)
    ring(0, 0)
    shared(1)
    partials(1)
    ring(1, 0)
    early = len(pending)
    last(2)
    multiply(2, 5, 6, 7)
    keep(2)
    launch(2)
    ring(0, 1)
    ring(1, 1)
    direction_send()
    ring(0, 2)
    ring(1, 2)
    settle(early)
    shared(3)
    ring(0, 3)
    partials(3)
    ring(3, 0)
    shared(2)
    ring(1, 3)
    partials(2)
    ring(2, 0)
    finish(0)
    deliver(0)
    ring(3, 1)
    ring(2, 1)
    finish(1)
    deliver(1)
    ring(3, 2)
    ring(2, 2)
    direction()
    ring(3, 3)
    ring(2, 3)
    received(0)
    finish(3)
    deliver(3)
    finish(2)
    deliver(2)
    received(1)
    received(3)
    received(2)
    settle(len(pending))


def per_device(latents, noise, noise_level, group_index, projections, upstream):
    weights = jnp.transpose(projections[0], (1, 0, 2))
    groups = group_index
    dma = pltpu.SemaphoreType.DMA
    vmem = pltpu.VMEM
    anywhere = pl.BlockSpec(memory_space=pl.ANY)
    direction, grads = pl.pallas_call(
        step_kernel,
        out_shape=(
            jax.ShapeDtypeStruct((32, 3072), BF16),
            jax.ShapeDtypeStruct((3, 160, 384), BF16),
        ),
        in_specs=[anywhere, anywhere, pl.BlockSpec(memory_space=pltpu.SMEM), anywhere, anywhere, anywhere],
        out_specs=(pl.BlockSpec(memory_space=pltpu.VMEM), pl.BlockSpec(memory_space=pltpu.VMEM)),
        scratch_shapes=[
            vmem((3, 5120, 384), BF16),
            vmem((4, 512, 1280), BF16),
            vmem((4, 256, 1280), BF16),
            vmem((4, 256, 1280), BF16),
            vmem((512, 384), F32),
            vmem((3, 512, 384), BF16),
            vmem((512, 384), BF16),
            vmem((1, 512), jnp.int32),
            vmem((512, 128), jnp.int32),
            vmem((512, 384), BF16),
            vmem((512, 1152), BF16),
            vmem((512, 1152), BF16),
            vmem((2, 1280, 512), BF16),
            vmem((1280, 512), BF16),
            vmem((512, 512), BF16),
            vmem((512, 512), BF16),
            vmem((1280, 1152), F32),
            vmem((2, 4, 160, 1152), BF16),
            vmem((2, 4, 160, 1152), BF16),
            vmem((160, 1152), BF16),
            vmem((160, 1152), BF16),
            vmem((2, 32, 3072), BF16),
            dma((3, 8, 2)), dma((3, 8)), dma((3,)), dma((3,)), dma((3,)),
            dma((4, 2)), dma((4, 2)), dma((4,)), dma((4,)),
            dma((4, 2)), dma((4,)), dma((2,)), dma((2,)),
            dma((6,)), dma((6,)), dma((4,)), dma((4,)),
            dma((2, 4, 4)), dma((2, 4, 2)), dma((6,)), dma((6, 2)),
            dma((2, 4, 2)), dma,
        ],
        compiler_params=pltpu.CompilerParams(
            collective_id=0, has_side_effects=True, vmem_limit_bytes=62 << 20
        ),
    )(latents[0], noise[0], noise_level, weights, upstream[0], groups)
    grads = jnp.transpose(grads.astype(F32), (1, 0, 2))
    return direction[None], grads


def solution(mesh):
    split = Mesh(
        mesh.devices.reshape(2, mesh.shape["seq"] // 2, 2, mesh.shape["fsdp"] // 2, 2), AXES
    )
    clip, heads = ("z", "yh"), ("x", "c")
    return jax.shard_map(
        per_device,
        mesh=split,
        in_specs=(
            P(clip, "m", None),
            P(clip, "m", None),
            P(clip),
            P(clip, None),
            P("m", clip, None, heads),
            P(clip, None, heads),
        ),
        out_specs=(P(clip, ("m", "x", "c"), None), P(("m", "z", "yh"), None, heads)),
        check_vma=False,
    )
```

time: 145 us -> 132 us (0.910); the launches traced: 145 us -> 130 us
  Pallas kernels: 139 us -> 125 us
    pallas_call x1, Pallas kernels: 139 us -> 125 us  [per_device(): pl.pallas_call(step_kernel, out_shape=(jax.ShapeDtypeStruct((32, 3072), B...]
where the time goes in v3:
time: 132 us; the launch traced here: 130 us
  Pallas kernels  125 us (95%)
  other arithmetic  1.9 us (1%)
  local copies, waits for them, and re-layouts  1.62 us (1%)
    pallas_call x1, Pallas kernels, per_device(): pl.pallas_call(step_kernel, out_shape=(jax.ShapeDtypeStruct((32, 3072), B...  125 us

profile of v3, /device:TPU:1, one launch (start us, length us, event | category | flops | bytes accessed | tf_op | source)
XLA Modules:
  0.0 129.8 jit_solution(8253243871241918519)
XLA Ops:
  1.3 125.0 %shard_map.77 = (bf16[32,3072]{1,0:T(8,128)(2,1)}, bf16[3,160,384]{2,1,0:T(8,128)(2,1)}) custom-call(bf16[256,5120]{1,0:T(8,128)(2,1)} %bitcast.9, bf16[256,5120]{1,0:T(8,128)(2,1)} %bitcast.10, f32[1]{0:T(128)S(6)} %copy.9.lvl_ref, bf16[3,320,384]{2,1,0:T(8,128)(2,1)} %bitcast.11, bf16[512,384]{1,0:T(8,128)(2,1)} %bitcast.12, s32[1,512]{1,0:T(1,128)} %gi_ref.1), custom_call_target="tpu_custom_call" | custom-call | tf_op jit(solution)/shard_map/pallas_call | solution.py:607
  126.3 1.9 %convert_bitcast_fusion = f32[160,3,384]{2,0,1:T(8,128)} fusion(bf16[3,160,384]{2,1,0:T(8,128)(2,1)} %get-tuple-element.5), kind=kLoop, calls=%fused_computation | loop fusion | flops 184320 | bytes 1105920 | tf_op jit(solution)/shard_map/transpose | solution.py:649
  128.2 1.6 %copy.10 = bf16[1,32,3072]{2,1,0:T(8,128)(2,1)} copy(bf16[1,32,3072]{2,1,0:T(8,128)(2,1)} %bitcast.13) | data formatting | bytes 393216

commit v4 on v3

--- a/solution.py
+++ b/solution.py
@@ -23,9 +23,9 @@
 def step_kernel(
     lat_ref, noi_ref, lvl_ref, proj_ref, up_ref, gi_ref,
     dir_ref, grad_ref,
-    wbuf, xbuf, latv, noiv, acc, tri, upb, gib, gcol, attb, cotb, coto,
+    wbuf, own, xbuf, latv, noiv, acc, tri, upb, gib, gcol, attb, cotb, coto,
     xts, xto, pbuf, dsbuf, gbuf, sbuf, rbuf, fbuf, obuf, dbuf,
-    wr, wc, ws, wcs, wos, ya, xa, xs, xxs, lsem, usem, xtr, xtss, cr, cs, er, es,
+    wr, wc, ws, wcs, wos, wl, ya, xa, xs, xxs, lsem, usem, xtr, xtss, cr, cs, er, es,
     rr, rs, fr, fs, dr, dsm,
 ):
     m, x, c, z, yh = (lax.axis_index(a) for a in AXES)
@@ -69,6 +69,12 @@
     def sent(ref, sem, cond=None):
         pending.append((lambda: wait_on(ref, sem), cond))
 
+    def only(cond, *calls):
+        @pl.when(cond)
+        def _():
+            for call, *arguments in calls:
+                call(*arguments)
+
     def settle(number):
         for wait, cond in pending[:number]:
             if cond is None:
@@ -86,22 +92,31 @@
     def w_rows(zb, core, i):
         return pl.ds(pl.multiple_of(zb * 640 + core * 320 + i * 160, 16), 160)
 
-    def own_rows(h, i, j):
-        return (
-            proj_ref.at[j, pl.ds(160 * i, 160), pl.ds(128 * h, 128)],
-            wbuf.at[h, w_rows(z, yh, i), pl.ds(128 * j, 128)],
-        )
-
-    every_own = [(h, i, j) for h in range(3) for i in range(2) for j in range(3)]
+    def own_chunk(h, i):
+        return wbuf.at[h, w_rows(z, yh, i), :]
+
+    def stage_own(h, i, dst, sem):
+        for j in range(3):
+            pltpu.make_async_copy(
+                proj_ref.at[j, pl.ds(160 * i, 160), pl.ds(128 * h, 128)],
+                dst.at[:, pl.ds(128 * j, 128)], sem,
+            ).start()
 
     @pl.when(home)
     def _():
-        for h, i, j in every_own:
-            pltpu.make_async_copy(*own_rows(h, i, j), wr.at[h, 0, i]).start()
-            if (i, j) == (1, 2) and h < 2:
+        for h in range(3):
+            for i in range(2):
+                stage_own(h, i, own_chunk(h, i), wr.at[h, 0, i])
+            if h < 2:
                 for p in (2 * h, 2 * h + 1):
                     read(p, 0).start()
                     read(p, 1).start()
+
+    @pl.when(away)
+    def _():
+        for h in range(3):
+            for i in range(2):
+                stage_own(h, i, own.at[h, i], wl.at[h, i])
 
     barrier = pltpu.get_barrier_semaphore()
     count = 0
@@ -124,9 +139,8 @@
 
     def w_turn(h):
         for i in range(2):
-            for j in range(3):
-                src, dst = own_rows(h, i, j)
-                go(rcopy(src, dst, wos.at[h], wr.at[h, 0, i], turn), away)
+            pl.when(away)(lambda: wait_on(own.at[h, i], wl.at[h, i]))
+            go(rcopy(own.at[h, i], own_chunk(h, i), wos.at[h], wr.at[h, 0, i], turn), away)
         sent(wbuf.at[h, 0:320, :], wos.at[h], away)
 
     w_turn(0)
@@ -281,11 +295,10 @@
 
     scale = 1.0 / math.sqrt(HEAD)
     fake = m == 1
-    def attend(h):
+    def attend(h, *blocks):
         qc, kc, vc = (pl.ds(j * 128, 128) for j in range(3))
-        dq = pl.ds(h * 384, 128)
         hc = pl.ds(h * 128, 128)
-        for b in range(4):
+        for b in blocks:
             nk = min(512, (b + 2) * 128)
             rows = pl.ds(b * 128, 128)
             s = dot(tri[h, rows, qc], tri[h, 0:nk, kc], ((1,), (1,))) * scale
@@ -302,7 +315,7 @@
                 dp = dot(upb[rows, hc], tri[h, 0:nk, vc], ((1,), (1,)))
                 inner = jnp.sum(p * dp, axis=-1, keepdims=True)
                 ds = (p * (dp - inner) * scale).astype(BF16)
-                cotb[rows, dq] = dot(ds, tri[h, 0:nk, kc], ((1,), (0,))).astype(BF16)
+                cotb[h * 3, rows, :] = dot(ds, tri[h, 0:nk, kc], ((1,), (0,))).astype(BF16)
                 pbuf[rows, 0:nk] = low
                 dsbuf[rows, 0:nk] = ds
 
@@ -317,25 +330,29 @@
                 first = max(0, (b - 1) * 128)
                 rows = pl.ds(first, 512 - first)
                 keys = pl.ds(b * 128, 128)
-                cotb[keys, pl.ds(h * 384 + j * 128, 128)] = dot(
+                cotb[h * 3 + j, keys, :] = dot(
                     left[rows, keys], right[rows, :], ((0,), (0,))
                 ).astype(BF16)
 
     parts = (
-        (0, 0, 256, False), (0, 256, 128, True),
-        (1, 384, 128, False), (1, 512, 256, True),
-        (2, 768, 256, False),
-        (3, 1024, 128, True),
+        (0, 0, 2, False), (0, 2, 1, True),
+        (1, 3, 1, False), (1, 4, 2, True),
+        (2, 6, 2, False),
+        (3, 8, 1, True),
     )
-    groups = ((0, 384), (384, 384), (768, 256), (1024, 128))
+    groups = ((0, 3), (3, 3), (6, 2), (8, 1))
+
+    def blocks_of(g):
+        return range(groups[g][0], groups[g][0] + groups[g][1])
+
+    def side_by_side(ref, g):
+        return jnp.concatenate([ref[p] for p in blocks_of(g)], axis=1)
 
     def spread(g):
-        for n, (pg, col, width, outer) in enumerate(parts):
+        for n, (pg, first, number, outer) in enumerate(parts):
             if pg == g:
-                piece = cotb.at[:, pl.ds(col, width)]
+                piece = cotb.at[pl.ds(first, number)]
                 send(rcopy(piece, piece, cs.at[n], cr.at[n], out if outer else sib), fake)
-
-    mine_cols = pl.ds(pl.multiple_of((x * 2 + yh) * 384, 128), 384)
 
     def direction_send():
         for dm in range(2):
@@ -343,7 +360,7 @@
                 for dc in range(2):
                     tm, tx, tc = lax.rem(m + dm, 2), lax.rem(x + dx, nx), lax.rem(c + dc, 2)
                     src = attb.at[pl.ds(pl.multiple_of((tm * 8 + tx * 2 + tc) * 32, 32), 32), :]
-                    dst = dbuf.at[m, :, mine_cols]
+                    dst = dbuf.at[m, x * 2 + yh]
                     sem = dr.at[dm, dx, yh]
                     cp = rcopy(src, dst, dsm, sem, at(m=tm, x=tx, c=tc, yh=c))
                     if dm + dx + dc == 0:
@@ -358,24 +375,24 @@
         sent(attb, dsm, away)
 
     def exchange(g, cond):
-        cols = pl.ds(*groups[g])
-        send(rcopy(cotb.at[:, cols], coto.at[:, cols], es.at[g], er.at[g], core_p), cond)
+        span = pl.ds(*groups[g])
+        send(rcopy(cotb.at[span], coto.at[span], es.at[g], er.at[g], core_p), cond)
 
     def arrived(g):
         @pl.when(m == 0)
         def _():
-            for n, (pg, col, width, _) in enumerate(parts):
+            for n, (pg, first, number, _) in enumerate(parts):
                 if pg == g:
-                    wait_on(cotb.at[:, pl.ds(col, width)], cr.at[n])
+                    wait_on(cotb.at[pl.ds(first, number)], cr.at[n])
 
     def partials(g):
-        cols = pl.ds(*groups[g])
-        wait_on(coto.at[:, cols], er.at[g])
+        wait_on(coto.at[pl.ds(*groups[g])], er.at[g])
+        mine, other = side_by_side(cotb, g), side_by_side(coto, g)
         for r in range(2):
             rows = pl.ds(r * 640, 640)
-            gbuf[rows, cols] = dot(xts[c, rows, :], cotb[:, cols], ((1,), (0,))) + dot(
-                xto[rows, :], coto[:, cols], ((1,), (0,))
-            )
+            both = dot(xts[c, rows, :], mine, ((1,), (0,))) + dot(xto[rows, :], other, ((1,), (0,)))
+            for n, p in enumerate(blocks_of(g)):
+                gbuf[p, rows, :] = both[:, n * 128 : (n + 1) * 128]
 
     def dest(o):
         return pl.multiple_of(lax.rem(z + nz + o, nz) * 160, 16)
@@ -384,51 +401,51 @@
         return pl.ds(80 * d, 80) if k == 0 else pl.ds(0, 160)
 
     def ring(g, k):
-        cols = pl.ds(*groups[g])
+        span = pl.ds(*groups[g])
         for d in range(2):
             o = (4 - k) if d == 0 else (k - 4)
             first = dest(o)
-            own, rest = pl.ds(80 * d, 80), pl.ds(80 - 80 * d, 80)
-            mine = gbuf[pl.ds(first + 80 * d, 80), cols]
+            mine, rest = pl.ds(80 * d, 80), pl.ds(80 - 80 * d, 80)
             if k >= 1:
-                wait_on(rbuf.at[d, k - 1, span_of(d, k - 1), cols], rr.at[d, g, k - 1])
-            if k == 0:
-                sbuf[d, k, own, cols] = mine.astype(BF16)
-            elif k == 1:
-                sbuf[d, k, own, cols] = (mine + rbuf[d, 0, own, cols].astype(F32)).astype(BF16)
-                sbuf[d, k, rest, cols] = gbuf[pl.ds(first + 80 - 80 * d, 80), cols].astype(BF16)
-            else:
-                sbuf[d, k, :, cols] = (
-                    gbuf[pl.ds(first, 160), cols] + rbuf[d, k - 1, :, cols].astype(F32)
-                ).astype(BF16)
-            piece = sbuf.at[d, k, span_of(d, k), cols]
-            cp = rcopy(
-                piece, rbuf.at[d, k, span_of(d, k), cols],
+                wait_on(rbuf.at[d, k - 1, span, span_of(d, k - 1), :], rr.at[d, g, k - 1])
+            for p in blocks_of(g):
+                if k == 0:
+                    sbuf[d, k, p, mine, :] = gbuf[p, pl.ds(first + 80 * d, 80), :].astype(BF16)
+                elif k == 1:
+                    sbuf[d, k, p, mine, :] = (
+                        gbuf[p, pl.ds(first + 80 * d, 80), :] + rbuf[d, 0, p, mine, :].astype(F32)
+                    ).astype(BF16)
+                    sbuf[d, k, p, rest, :] = gbuf[p, pl.ds(first + 80 - 80 * d, 80), :].astype(BF16)
+                else:
+                    sbuf[d, k, p, :, :] = (
+                        gbuf[p, pl.ds(first, 160), :] + rbuf[d, k - 1, p, :, :].astype(F32)
+                    ).astype(BF16)
+            go(rcopy(
+                sbuf.at[d, k, span, span_of(d, k), :], rbuf.at[d, k, span, span_of(d, k), :],
                 rs.at[d, g, min(k, 1)], rr.at[d, g, k], up_z if d == 0 else dn_z,
-            )
-            if k == 0:
-                send(cp)
-            else:
-                go(cp)
-        if k == 3:
-            for d in range(2):
-                sent(sbuf.at[d, 1:4, :, cols], rs.at[d, g, 1])
+            ))
+
+    def ring_sent(g):
+        span = pl.ds(*groups[g])
+        for d in range(2):
+            wait_on(sbuf.at[d, 0, span, span_of(d, 0), :], rs.at[d, g, 0])
+            wait_on(sbuf.at[d, 1:4, span, :, :], rs.at[d, g, 1])
 
     def finish(g):
-        cols = pl.ds(*groups[g])
         for d in range(2):
-            wait_on(rbuf.at[d, 3, :, cols], rr.at[d, g, 3])
-        fbuf[:, cols] = (
-            gbuf[pl.ds(dest(0), 160), cols]
-            + (rbuf[0, 3, :, cols].astype(F32) + rbuf[1, 3, :, cols].astype(F32))
-        ).astype(BF16)
+            wait_on(rbuf.at[d, 3, pl.ds(*groups[g]), :, :], rr.at[d, g, 3])
+        for p in blocks_of(g):
+            fbuf[p] = (
+                gbuf[p, pl.ds(dest(0), 160), :]
+                + (rbuf[0, 3, p].astype(F32) + rbuf[1, 3, p].astype(F32))
+            ).astype(BF16)
 
     def deliver(g):
-        for n, (pg, col, width, outer) in enumerate(parts):
+        for n, (pg, first, number, outer) in enumerate(parts):
             if pg != g:
                 continue
-            piece = fbuf.at[:, pl.ds(col, width)]
-            dst = obuf.at[:, pl.ds(col, width)]
+            piece = fbuf.at[pl.ds(first, number)]
+            dst = obuf.at[pl.ds(first, number)]
             straight = (m == 1) if outer else (m <= 1)
             send(rcopy(piece, dst, fs.at[n, 0], fr.at[n], turn), jnp.logical_and(straight, away))
 
@@ -440,140 +457,149 @@
                 send(rcopy(piece, dst, fs.at[n, 1], fr.at[n], at(c=1 - yh, yh=c)), m == 0)
 
     def received(g):
-        for n, (pg, col, width, _) in enumerate(parts):
+        for n, (pg, first, number, _) in enumerate(parts):
             if pg == g:
-                wait_on(obuf.at[:, pl.ds(col, width)], fr.at[n])
-                for k in range(width // 128):
-                    p = col // 128 + k
-                    grad_ref[p % 3, :, pl.ds(p // 3 * 128, 128)] = obuf[:, pl.ds(p * 128, 128)]
+                wait_on(obuf.at[pl.ds(first, number)], fr.at[n])
+                for p in range(first, first + number):
+                    grad_ref[p % 3, :, pl.ds(p // 3 * 128, 128)] = obuf[p]
 
     def direction():
         for dm in range(2):
             for dx in range(4):
                 for b in range(2):
-                    wait_on(
-                        dbuf.at[lax.rem(m + dm, 2), :, pl.ds(pl.multiple_of((lax.rem(x + nx - dx, nx) * 2 + b) * 384, 128), 384)],
-                        dr.at[dm, dx, b],
-                    )
-        dir_ref[...] = (dbuf[1].astype(F32) - dbuf[0].astype(F32)).astype(BF16)
+                    wait_on(dbuf.at[lax.rem(m + dm, 2), lax.rem(x + nx - dx, nx) * 2 + b], dr.at[dm, dx, b])
+        for n in range(8):
+            dir_ref[:, pl.ds(n * 384, 384)] = (dbuf[1, n].astype(F32) - dbuf[0, n].astype(F32)).astype(BF16)
 
     def shared(g):
         arrived(g)
         exchange(g, m == 0)
 
-    def launch(h):
-        attend(h)
+    def values_done(h):
         key_side(h, 2)
         if h == 2:
             spread(3)
             exchange(3, fake)
+
+    def keys_done(h):
         key_side(h, 1)
         spread(h)
         exchange(h, fake)
 
+    w_event(0, 0, 0, home)
+    w_event(0, 0, 1, home)
     noise(0)
     x_own(0)
-    w_event(0, 0, 0, home)
-    w_event(0, 0, 1, home)
-    w_event(1, 0, 0, home)
-    w_event(1, 0, 1, home)
     noise(1)
-    x_own(1)
     w_event(0, 0, 0, away)
     w_event(0, 0, 1, away)
     w_turn(1)
     stage(0, 1, 0)
+    w_event(1, 0, 0, home)
+    w_event(1, 0, 1, home)
+    x_own(1)
     x_y(0)
+    noise(2)
+    stage(0, 1, 1)
     w_event(2, 0, 0, home)
-    noise(2)
+    w_event(2, 0, 1, home)
+    w_turn(2)
     x_own(2)
-    stage(0, 1, 1)
-    w_event(2, 0, 1, home)
     x_y(1)
     stage(0, 2, 0)
-    w_turn(2)
     w_event(1, 0, 0, away)
-    x_z(0)
     noise(3)
     x_own(3)
+    x_z(0)
     stage(0, 2, 1)
     w_event(1, 0, 1, away)
     x_y(2)
     stage(0, 3, 0)
     x_z(1)
     stage(0, 3, 1)
-    side_inputs()
     x_ready(0)
     turned(0)
     last(0)
     stage(1, 1, 0)
     x_y(3)
     x_z(2)
-    multiply_columns(0)
+    stage(1, 1, 1)
+    side_inputs()
+    x_ready(1)
+    turned(1)
     turned_send(0)
-    stage(1, 1, 1)
-    x_z(3)
-    x_ready(1)
-    multiply_columns(1)
-    turned(1)
     stage(1, 2, 0)
     w_event(2, 0, 0, away)
+    multiply_columns(0)
+    multiply_columns(1)
+    stage(1, 2, 1)
+    w_event(2, 0, 1, away)
+    x_z(3)
     x_ready(2)
     multiply_columns(2)
     turned(2)
     turned_send(1)
-    stage(1, 2, 1)
-    w_event(2, 0, 1, away)
+    stage(1, 3, 0)
     x_ready(3)
     multiply_columns(3)
     keep(0)
-    stage(1, 3, 0)
-    multiply(1, 0, 1)
     stage(1, 3, 1)
+    stage(2, 1, 0)
     attention_inputs()
-    launch(0)
+    attend(0, 0, 1)
+    multiply(1, 0, 1, 2)
+    last(1)
+    attend(0, 2, 3)
+    values_done(0)
+    keys_done(0)
+    stage(2, 1, 1)
+    multiply(1, 3, 4, 5, 6, 7)
+    keep(1)
+    stage(2, 2, 0)
+    attend(1, 0, 1)
+    stage(2, 2, 1)
+    attend(1, 2, 3)
+    values_done(1)
+    keys_done(1)
+    stage(2, 3, 0)
     turned(3)
     turned_send(2)
     turned_send(3)
-    last(1)
-    multiply(1, 2, 3, 4)
-    stage(2, 1, 0)
-    multiply(1, 5, 6, 7)
-    keep(1)
-    stage(2, 1, 1)
-    launch(1)
-    stage(2, 2, 0)
-    multiply(2, 0)
+    multiply(2, 0, 1, 2)
+    stage(2, 3, 1)
     for q in range(2):
         wait_on(xto.at[pl.ds(q * 640, 640), :], xtr.at[q])
     shared(0)
-    stage(2, 2, 1)
-    multiply(2, 1, 2)
     partials(0)
-    stage(2, 3, 0)
+    ring(0, 0)
     multiply(2, 3, 4)
-    stage(2, 3, 1)
-    ring(0, 0)
-    shared(1)
-    partials(1)
-    ring(1, 0)
+    teacher = m == 0
+    only(fake, (partials, 1), (ring, 1, 0))
     early = len(pending)
     last(2)
     multiply(2, 5, 6, 7)
     keep(2)
-    launch(2)
     ring(0, 1)
-    ring(1, 1)
+    attend(2, 0, 1)
+    only(fake, (ring, 1, 1))
+    attend(2, 2, 3)
+    values_done(2)
+    keys_done(2)
+    shared(1)
+    only(teacher, (partials, 1), (ring, 1, 0))
+    ring(0, 2)
+    only(teacher, (ring, 1, 1))
+    only(fake, (ring, 1, 2))
+    ring(0, 3)
     direction_send()
-    ring(0, 2)
-    ring(1, 2)
+    only(teacher, (ring, 1, 2))
+    only(fake, (ring, 1, 3))
     settle(early)
     shared(3)
-    ring(0, 3)
     partials(3)
     ring(3, 0)
+    only(teacher, (ring, 1, 3))
     shared(2)
-    ring(1, 3)
     partials(2)
     ring(2, 0)
     finish(0)
@@ -594,8 +620,15 @@
     deliver(2)
     received(1)
     received(3)
+    for g in range(4):
+        ring_sent(g)
     received(2)
     settle(len(pending))
+
+
+def widen_kernel(direction_ref, grads_ref, direction_out, grads_out):
+    direction_out[...] = direction_ref[...]
+    grads_out[...] = grads_ref[...].astype(F32)
 
 
 def per_device(latents, noise, noise_level, group_index, projections, upstream):
@@ -614,6 +647,7 @@
         out_specs=(pl.BlockSpec(memory_space=pltpu.VMEM), pl.BlockSpec(memory_space=pltpu.VMEM)),
         scratch_shapes=[
             vmem((3, 5120, 384), BF16),
+            vmem((3, 2, 160, 384), BF16),
             vmem((4, 512, 1280), BF16),
             vmem((4, 256, 1280), BF16),
             vmem((4, 256, 1280), BF16),
@@ -623,19 +657,19 @@
             vmem((1, 512), jnp.int32),
             vmem((512, 128), jnp.int32),
             vmem((512, 384), BF16),
-            vmem((512, 1152), BF16),
-            vmem((512, 1152), BF16),
+            vmem((9, 512, 128), BF16),
+            vmem((9, 512, 128), BF16),
             vmem((2, 1280, 512), BF16),
             vmem((1280, 512), BF16),
             vmem((512, 512), BF16),
             vmem((512, 512), BF16),
-            vmem((1280, 1152), F32),
-            vmem((2, 4, 160, 1152), BF16),
-            vmem((2, 4, 160, 1152), BF16),
-            vmem((160, 1152), BF16),
-            vmem((160, 1152), BF16),
-            vmem((2, 32, 3072), BF16),
-            dma((3, 8, 2)), dma((3, 8)), dma((3,)), dma((3,)), dma((3,)),
+            vmem((9, 1280, 128), F32),
+            vmem((2, 4, 9, 160, 128), BF16),
+            vmem((2, 4, 9, 160, 128), BF16),
+            vmem((9, 160, 128), BF16),
+            vmem((9, 160, 128), BF16),
+            vmem((2, 8, 32, 384), BF16),
+            dma((3, 8, 2)), dma((3, 8)), dma((3,)), dma((3,)), dma((3,)), dma((3, 2)),
             dma((4, 2)), dma((4, 2)), dma((4,)), dma((4,)),
             dma((4, 2)), dma((4,)), dma((2,)), dma((2,)),
             dma((6,)), dma((6,)), dma((4,)), dma((4,)),
@@ -646,8 +680,16 @@
             collective_id=0, has_side_effects=True, vmem_limit_bytes=62 << 20
         ),
     )(latents[0], noise[0], noise_level, weights, upstream[0], groups)
-    grads = jnp.transpose(grads.astype(F32), (1, 0, 2))
-    return direction[None], grads
+    direction, grads = pl.pallas_call(
+        widen_kernel,
+        out_shape=(
+            jax.ShapeDtypeStruct((32, 3072), BF16),
+            jax.ShapeDtypeStruct((3, 160, 384), F32),
+        ),
+        in_specs=[pl.BlockSpec(memory_space=pltpu.VMEM)] * 2,
+        out_specs=(pl.BlockSpec(memory_space=pltpu.VMEM), pl.BlockSpec(memory_space=pltpu.VMEM)),
+    )(direction, grads)
+    return direction[None], jnp.transpose(grads, (1, 0, 2))
 
 
 def solution(mesh):

time: 132 us -> 127 us (0.962); the launches traced: 130 us -> 127 us
  other arithmetic: 1.9 us -> 0 us
  local copies, waits for them, and re-layouts: 1.62 us -> 0 us
    pallas_call x0 -> x1, Pallas kernels: none -> 2.04 us  [per_device(): pl.pallas_call(widen_kernel, out_shape=(jax.ShapeDtypeStruct((32, 3072),...]
    transpose x1 -> x0, other arithmetic: 1.9 us -> none  [per_device(): grads = jnp.transpose(grads.astype(F32), (1, 0, 2))]
    unnamed x1 -> x0, local copies, waits for them, and re-layouts: 1.62 us -> none
    pallas_call x1, Pallas kernels: 125 us -> 124 us  [per_device(): pl.pallas_call(step_kernel, out_shape=(jax.ShapeDtypeStruct((32, 3072), B...]
where the time goes in v4:
time: 127 us
  Pallas kernels  126 us (99%)
  between operations  1.28 us (1%)
    pallas_call x1, Pallas kernels, per_device(): pl.pallas_call(step_kernel, out_shape=(jax.ShapeDtypeStruct((32, 3072), B...  124 us

profile of v4, /device:TPU:1, one launch (start us, length us, event | category | flops | bytes accessed | tf_op | source)
XLA Modules:
  0.0 126.8 jit_solution(1816698471305349634)
XLA Ops:
  1.3 123.5 %shard_map.77 = (bf16[32,3072]{1,0:T(8,128)(2,1)}, bf16[3,160,384]{2,1,0:T(8,128)(2,1)}) custom-call(bf16[256,5120]{1,0:T(8,128)(2,1)} %bitcast.8, bf16[256,5120]{1,0:T(8,128)(2,1)} %bitcast.9, f32[1]{0:T(128)S(6)} %copy.8.lvl_ref, bf16[3,320,384]{2,1,0:T(8,128)(2,1)} %bitcast.10, bf16[512,384]{1,0:T(8,128)(2,1)} %bitcast.11, s32[1,512]{1,0:T(1,128)} %gi_ref.1), custom_call_target="tpu_custom_call" | custom-call | tf_op jit(solution)/shard_map/pallas_call | solution.py:640
  124.8 2.0 %shard_map.78 = (bf16[32,3072]{1,0:T(8,128)(2,1)}, f32[3,160,384]{2,1,0:T(8,128)}) custom-call(bf16[32,3072]{1,0:T(8,128)(2,1)} %get-tuple-element.6.direction_ref, bf16[3,160,384]{2,1,0:T(8,128)(2,1)} %get-tuple-element.7.grads_ref), custom_call_target="tpu_custom_call" | custom-call | tf_op jit(solution)/shard_map/pallas_call | solution.py:683

commit v5 on v4

--- a/solution.py
+++ b/solution.py
@@ -295,7 +295,7 @@
 
     scale = 1.0 / math.sqrt(HEAD)
     fake = m == 1
-    def attend(h, *blocks):
+    def attention(h, blocks, backward):
         qc, kc, vc = (pl.ds(j * 128, 128) for j in range(3))
         hc = pl.ds(h * 128, 128)
         for b in blocks:
@@ -309,15 +309,19 @@
             p = w * (1.0 / jnp.sum(w, axis=-1, keepdims=True))
             low = p.astype(BF16)
             attb[rows, hc] = dot(low, tri[h, 0:nk, vc], ((1,), (0,))).astype(BF16)
-
-            @pl.when(fake)
-            def _():
+            if backward:
+                pbuf[rows, 0:nk] = low
                 dp = dot(upb[rows, hc], tri[h, 0:nk, vc], ((1,), (1,)))
                 inner = jnp.sum(p * dp, axis=-1, keepdims=True)
                 ds = (p * (dp - inner) * scale).astype(BF16)
+                dsbuf[rows, 0:nk] = ds
                 cotb[h * 3, rows, :] = dot(ds, tri[h, 0:nk, kc], ((1,), (0,))).astype(BF16)
-                pbuf[rows, 0:nk] = low
-                dsbuf[rows, 0:nk] = ds
+
+    teacher = m == 0
+
+    def attend(h, *blocks):
+        only(fake, (attention, h, blocks, True))
+        only(teacher, (attention, h, blocks, False))
 
     def key_side(h, j):
         left, right = (
@@ -573,35 +577,32 @@
     partials(0)
     ring(0, 0)
     multiply(2, 3, 4)
-    teacher = m == 0
     only(fake, (partials, 1), (ring, 1, 0))
     early = len(pending)
     last(2)
-    multiply(2, 5, 6, 7)
-    keep(2)
+    only(fake, (multiply, 2, 5, 6, 7), (keep, 2))
     ring(0, 1)
-    attend(2, 0, 1)
-    only(fake, (ring, 1, 1))
-    attend(2, 2, 3)
+    shared(1)
+    only(fake, (attention, 2, (0, 1), True), (ring, 1, 1), (attention, 2, (2, 3), True))
     values_done(2)
     keys_done(2)
-    shared(1)
     only(teacher, (partials, 1), (ring, 1, 0))
     ring(0, 2)
-    only(teacher, (ring, 1, 1))
+    only(teacher, (multiply, 2, 5, 6, 7), (keep, 2), (attention, 2, (0, 1), False), (ring, 1, 1))
+    only(teacher, (attention, 2, (2, 3), False))
     only(fake, (ring, 1, 2))
     ring(0, 3)
-    direction_send()
+    shared(3)
     only(teacher, (ring, 1, 2))
+    shared(2)
     only(fake, (ring, 1, 3))
-    settle(early)
-    shared(3)
     partials(3)
     ring(3, 0)
-    only(teacher, (ring, 1, 3))
-    shared(2)
     partials(2)
     ring(2, 0)
+    only(teacher, (ring, 1, 3))
+    direction_send()
+    settle(early)
     finish(0)
     deliver(0)
     ring(3, 1)

time: 127 us -> 123 us (0.969)
  Pallas kernels: 126 us -> 121 us
    pallas_call x1, Pallas kernels: 124 us -> 119 us  [per_device(): pl.pallas_call(step_kernel, out_shape=(jax.ShapeDtypeStruct((32, 3072), B...]
where the time goes in v5:
time: 123 us
  Pallas kernels  121 us (98%)
  between operations  1.28 us (1%)
    pallas_call x1, Pallas kernels, per_device(): pl.pallas_call(step_kernel, out_shape=(jax.ShapeDtypeStruct((32, 3072), B...  119 us

profile of v5, /device:TPU:1, one launch (start us, length us, event | category | flops | bytes accessed | tf_op | source)
XLA Modules:
  0.0 122.6 jit_solution(9172805445074640067)
XLA Ops:
  1.3 119.3 %shard_map.77 = (bf16[32,3072]{1,0:T(8,128)(2,1)}, bf16[3,160,384]{2,1,0:T(8,128)(2,1)}) custom-call(bf16[256,5120]{1,0:T(8,128)(2,1)} %bitcast.8, bf16[256,5120]{1,0:T(8,128)(2,1)} %bitcast.9, f32[1]{0:T(128)S(6)} %copy.8.lvl_ref, bf16[3,320,384]{2,1,0:T(8,128)(2,1)} %bitcast.10, bf16[512,384]{1,0:T(8,128)(2,1)} %bitcast.11, s32[1,512]{1,0:T(1,128)} %gi_ref.1), custom_call_target="tpu_custom_call" | custom-call | tf_op jit(solution)/shard_map/pallas_call | solution.py:641
  120.6 2.0 %shard_map.78 = (bf16[32,3072]{1,0:T(8,128)(2,1)}, f32[3,160,384]{2,1,0:T(8,128)}) custom-call(bf16[32,3072]{1,0:T(8,128)(2,1)} %get-tuple-element.6.direction_ref, bf16[3,160,384]{2,1,0:T(8,128)(2,1)} %get-tuple-element.7.grads_ref), custom_call_target="tpu_custom_call" | custom-call | tf_op jit(solution)/shard_map/pallas_call | solution.py:684

commit v6 on v5

--- a/solution.py
+++ b/solution.py
@@ -365,7 +365,7 @@
                     tm, tx, tc = lax.rem(m + dm, 2), lax.rem(x + dx, nx), lax.rem(c + dc, 2)
                     src = attb.at[pl.ds(pl.multiple_of((tm * 8 + tx * 2 + tc) * 32, 32), 32), :]
                     dst = dbuf.at[m, x * 2 + yh]
-                    sem = dr.at[dm, dx, yh]
+                    sem = dr
                     cp = rcopy(src, dst, dsm, sem, at(m=tm, x=tx, c=tc, yh=c))
                     if dm + dx + dc == 0:
                         go(cp, away)
@@ -426,14 +426,13 @@
                     ).astype(BF16)
             go(rcopy(
                 sbuf.at[d, k, span, span_of(d, k), :], rbuf.at[d, k, span, span_of(d, k), :],
-                rs.at[d, g, min(k, 1)], rr.at[d, g, k], up_z if d == 0 else dn_z,
+                rs.at[g, min(k, 1)], rr.at[d, g, k], up_z if d == 0 else dn_z,
             ))
 
     def ring_sent(g):
         span = pl.ds(*groups[g])
-        for d in range(2):
-            wait_on(sbuf.at[d, 0, span, span_of(d, 0), :], rs.at[d, g, 0])
-            wait_on(sbuf.at[d, 1:4, span, :, :], rs.at[d, g, 1])
+        wait_on(sbuf.at[0, 0, span, :, :], rs.at[g, 0])
+        wait_on(sbuf.at[:, 1:4, span, :, :], rs.at[g, 1])
 
     def finish(g):
         for d in range(2):
@@ -468,10 +467,7 @@
                     grad_ref[p % 3, :, pl.ds(p // 3 * 128, 128)] = obuf[p]
 
     def direction():
-        for dm in range(2):
-            for dx in range(4):
-                for b in range(2):
-                    wait_on(dbuf.at[lax.rem(m + dm, 2), lax.rem(x + nx - dx, nx) * 2 + b], dr.at[dm, dx, b])
+        wait_on(dbuf, dr)
         for n in range(8):
             dir_ref[:, pl.ds(n * 384, 384)] = (dbuf[1, n].astype(F32) - dbuf[0, n].astype(F32)).astype(BF16)
 
@@ -674,8 +670,8 @@
             dma((4, 2)), dma((4, 2)), dma((4,)), dma((4,)),
             dma((4, 2)), dma((4,)), dma((2,)), dma((2,)),
             dma((6,)), dma((6,)), dma((4,)), dma((4,)),
-            dma((2, 4, 4)), dma((2, 4, 2)), dma((6,)), dma((6, 2)),
-            dma((2, 4, 2)), dma,
+            dma((2, 4, 4)), dma((4, 2)), dma((6,)), dma((6, 2)),
+            dma, dma,
         ],
         compiler_params=pltpu.CompilerParams(
             collective_id=0, has_side_effects=True, vmem_limit_bytes=62 << 20

time: 123 us -> 122 us (level)
  no operation moved by 1% of the time
where the time goes in v6:
time: 122 us
  Pallas kernels  121 us (99%)
  between operations  1.28 us (1%)
    pallas_call x1, Pallas kernels, per_device(): pl.pallas_call(step_kernel, out_shape=(jax.ShapeDtypeStruct((32, 3072), B...  119 us

profile of v6, /device:TPU:1, one launch (start us, length us, event | category | flops | bytes accessed | tf_op | source)
XLA Modules:
  0.0 122.4 jit_solution(13632462775419484742)
XLA Ops:
  1.3 119.1 %shard_map.77 = (bf16[32,3072]{1,0:T(8,128)(2,1)}, bf16[3,160,384]{2,1,0:T(8,128)(2,1)}) custom-call(bf16[256,5120]{1,0:T(8,128)(2,1)} %bitcast.8, bf16[256,5120]{1,0:T(8,128)(2,1)} %bitcast.9, f32[1]{0:T(128)S(6)} %copy.8.lvl_ref, bf16[3,320,384]{2,1,0:T(8,128)(2,1)} %bitcast.10, bf16[512,384]{1,0:T(8,128)(2,1)} %bitcast.11, s32[1,512]{1,0:T(1,128)} %gi_ref.1), custom_call_target="tpu_custom_call" | custom-call | tf_op jit(solution)/shard_map/pallas_call | solution.py:637
  120.4 2.0 %shard_map.78 = (bf16[32,3072]{1,0:T(8,128)(2,1)}, f32[3,160,384]{2,1,0:T(8,128)}) custom-call(bf16[32,3072]{1,0:T(8,128)(2,1)} %get-tuple-element.6.direction_ref, bf16[3,160,384]{2,1,0:T(8,128)(2,1)} %get-tuple-element.7.grads_ref), custom_call_target="tpu_custom_call" | custom-call | tf_op jit(solution)/shard_map/pallas_call | solution.py:680
